TPU v7x, 32 devices: a whole 2x2x4 slice. The times are simulated.
32 devices in a mesh: tm: 4 (over z), space: 4 (over y, core), net: 2 (over x).
Axes of the slice: x: 2, y: 2, z: 4, core: 2. Of those that a mesh axis runs over, the one named last changes fastest.
Arguments:
- query_rows: bfloat16 [2, 4, 8, 64, 2560], P('net', 'tm', 'space'), may hold values from -140 to 140
- key_rows: bfloat16 [2, 4, 8, 64, 2560], P('net', 'tm', 'space'), may hold values from -8 to 8
- value_rows: bfloat16 [2, 4, 8, 64, 2560], P('net', 'tm', 'space'), may hold values from -6 to 6
- time_proj: bfloat16 [2, 256, 2560], P('net'), may hold values from -0.375 to 0.375
- block_list: int32 [4, 8, 9], P('tm', 'space'), may hold values from 0 to 31, as said below
- block_count: int32 [4, 8], P('tm', 'space'), may hold values from 1 to 9
- timestep: int32 [1], replicated, may hold values from 0 to 999
Outputs:
- latent_grad: bfloat16 [4, 8, 64, 2560], P('tm', 'space', None, 'net')
Inputs may be any that keep to these rules, and one draw needn't show every extreme that they name: `block_list`: entry (f, b, s) names a block f2 * 8 + b2 with f2 within one of f and b2 within one of b, inside the grid; slot 0 is the query's own block; the first block_count[f, b] entries are distinct; the rest repeat the own block.
All inputs are finite; a program needn't handle non-finite values.
Results may differ from a plain program's by a relative error of at most 0.0053.
Values may be sent and summed in bfloat16 or wider, within the bound.
No kernel may reach another device: no remote copies, remote signals or barrier semaphores. Data moves between devices by JAX's collectives and lax.ppermute only.
A program may use at most 64 MiB of HBM per device.

v0:
```python
import jax
import jax.numpy as jnp
from jax import lax
from jax.experimental import pallas as pl
from jax.experimental.pallas import tpu as pltpu
from jax.sharding import PartitionSpec as P


HD = 128
FREQ = 256
DEAD = -1e30
VMEM_LIMIT = 20 << 20


def side_by_side(arrays):
    return jnp.stack(arrays, axis=1)


def swaps(count, first):
    pairs = [(i, i + 1) for i in range(first, count - 1, 2)]
    return pairs + [(b, a) for a, b in pairs]


def time_feature(timestep):
    half = FREQ // 2
    freqs = jnp.exp(-jnp.log(jnp.float32(10000.0)) * jnp.arange(half, dtype=jnp.float32) / half)
    angle = timestep[0].astype(jnp.float32) * freqs
    return jax.nn.silu(jnp.concatenate([jnp.cos(angle), jnp.sin(angle)])).astype(jnp.bfloat16)[None, :]


def attend(scalars_ref, live_ref, feature_ref, proj_ref, q_ref, k_ref, v_ref, own_cross_ref, own_chip_ref,
           frames, out_ref):
    width = out_ref.shape[-1]
    block_len = q_ref.shape[1]
    base, sign = scalars_ref[0], scalars_ref[1].astype(jnp.float32)
    feature = jnp.broadcast_to(feature_ref[...], (16, feature_ref.shape[-1]))
    lane = lax.broadcasted_iota(jnp.int32, (1, 2 * block_len), 1)
    dead = [
        jnp.where(jnp.where(lane < block_len, live_ref[2 * at], live_ref[2 * at + 1]) > 0, 0.0, DEAD)
        for at in range(4 * (1 + len(frames)))
    ]
    for head in range(width // HD):
        here = slice(head * HD, (head + 1) * HD)
        there = pl.ds(pl.multiple_of(base + head * HD, HD), HD)

        def rows(side, own_ref):
            parts = [own_ref[0, :, there], own_ref[1, :, there],
                     own_cross_ref[side, :, there], own_chip_ref[side, :, there]]
            for blocks in frames:
                parts += blocks(side, here)
            return jnp.concatenate(parts, axis=0)

        queries = jnp.concatenate([q_ref[0, :, there], q_ref[1, :, there]], axis=0)
        scores = lax.dot_general(
            rows(0, k_ref), queries, (((1,), (1,)), ((), ())), preferred_element_type=jnp.float32
        )
        scores = scores * HD ** (-0.5)
        scores = jnp.concatenate(
            [scores[at * block_len:(at + 1) * block_len] + row for at, row in enumerate(dead)], axis=0
        )
        expo = jnp.exp(scores - jnp.max(scores, axis=0, keepdims=True))
        total = jnp.sum(expo, axis=0, keepdims=True)
        mixed = lax.dot_general(
            expo.astype(jnp.bfloat16), rows(1, v_ref), (((0,), (0,)), ((), ())),
            preferred_element_type=jnp.float32,
        )
        total = jnp.transpose(jnp.broadcast_to(total, (8, 2 * block_len)))[:, 0:1]
        gate = sign * jnp.dot(feature, proj_ref[:, there], preferred_element_type=jnp.float32)[0:1]
        mixed = mixed / total * gate
        out_ref[0, :, here] = mixed[:block_len].astype(out_ref.dtype)
        out_ref[1, :, here] = mixed[block_len:].astype(out_ref.dtype)


def attention(kernel, operands, width, dtype, keys_seen):
    queries = operands[4]
    blocks, block_len, _ = queries.shape
    vmem, smem = (pl.BlockSpec(memory_space=space) for space in (pltpu.VMEM, pltpu.SMEM))
    return pl.pallas_call(
        kernel,
        out_shape=jax.ShapeDtypeStruct((blocks, block_len, width), dtype),
        in_specs=[smem, smem] + [vmem] * (len(operands) - 2),
        out_specs=vmem,
        cost_estimate=pl.CostEstimate(
            flops=4 * blocks * block_len * keys_seen * width,
            bytes_accessed=4 * keys_seen * width,
            transcendentals=blocks * block_len * keys_seen * width // HD,
        ),
        compiler_params=pltpu.CompilerParams(vmem_limit_bytes=VMEM_LIMIT),
    )(*operands)


def attend_away(scalars, live, feature, proj, q, k, v, own_cross, own_chip, even, odd, cross, chip, out):
    def frame(at, near):
        return lambda side, here: [near[side, 0, :, here], near[side, 1, :, here],
                                   cross[side, at, :, here], chip[side, at, :, here]]

    attend(scalars, live, feature, proj, q, k, v, own_cross, own_chip, (frame(0, even), frame(1, odd)), out)


def attend_kept(scalars, live, feature, proj, q, k, v, own_cross, own_chip,
                even_edge, odd_edge, even_inner, odd_inner, cross, chip, out):
    def frame(at, edge, inner):
        return lambda side, here: [edge[side, :, here], inner[side, :, here],
                                   cross[side, at, :, here], chip[side, at, :, here]]

    frames = (frame(0, even_edge, even_inner), frame(1, odd_edge, odd_inner))
    attend(scalars, live, feature, proj, q, k, v, own_cross, own_chip, frames, out)


def shards(query_rows, key_rows, value_rows, time_proj, block_list, block_count, timestep):
    queries, keys, values = query_rows[0, 0], key_rows[0, 0], value_rows[0, 0]
    blocks_here, block_len, features = queries.shape
    assert query_rows.shape[1] == 1 and blocks_here == 2
    width = features // lax.axis_size("net")
    frame, space, net = lax.axis_index("tm"), lax.axis_index("space"), lax.axis_index("net")
    frames, total_blocks = lax.axis_size("tm"), blocks_here * lax.axis_size("space")
    odd = space % 2
    time_pairs = {"even": swaps(frames, 0), "odd": swaps(frames, 1)}
    chip_pairs, cross_pairs = (swaps(lax.axis_size("space"), first) for first in (0, 1))

    def piece(which, half):
        start = (which, 0, half * width)
        return jnp.stack([
            lax.dynamic_slice(x, start, (1, block_len, width))[0] for x in (keys, values)
        ])

    def whole(which):
        return jnp.stack([lax.dynamic_index_in_dim(x, which, 0, keepdims=False) for x in (keys, values)])

    other = 1 - net
    sent = jnp.stack([piece(odd, other), piece(1 - odd, other)], axis=1)
    first = [lax.ppermute(sent, "tm", time_pairs[turn]) for turn in time_pairs]
    own_cross = lax.ppermute(whole(odd), "space", cross_pairs)
    own_chip = lax.ppermute(whole(1 - odd), "space", chip_pairs)
    edge_sent, inner_sent = piece(odd, net), piece(1 - odd, net)
    edges = [lax.ppermute(edge_sent, "tm", time_pairs[turn]) for turn in time_pairs]
    inners = [lax.ppermute(inner_sent, "tm", time_pairs[turn]) for turn in time_pairs]

    step = 1 - 2 * (frame % 2)
    side = 2 * odd - 1
    edge_at, inner_at = 2 * space + odd, 2 * space + 1 - odd
    cross_at, chip_at = edge_at + side, inner_at - side
    at_block = jnp.stack([2 * space, 2 * space + 1, cross_at, chip_at] + [edge_at, inner_at, cross_at, chip_at] * 2)
    at_frame = jnp.stack([frame] * 4 + [frame + step] * 4 + [frame - step] * 4)
    inside = (at_frame >= 0) & (at_frame < frames) & (at_block >= 0) & (at_block < total_blocks)
    name = jnp.where(inside, at_frame * total_blocks + at_block, -1)
    listed = block_list.reshape(blocks_here, -1)
    slots = jnp.arange(listed.shape[-1], dtype=jnp.int32)
    listed = jnp.where(slots[None, :] < block_count.reshape(blocks_here, 1), listed, -2)
    live = jnp.any(listed[None, :, :] == name[:, None, None], axis=-1).astype(jnp.int32).reshape(-1)

    feature, proj = time_feature(timestep), time_proj[0]
    sign = 2 * net - 1
    shared = (feature, proj, queries, keys, values, own_cross, own_chip)
    keys_seen = name.shape[0] * block_len

    first_cross = lax.ppermute(jnp.stack([x[:, 0] for x in first], axis=1), "space", cross_pairs)
    first_chip = lax.ppermute(jnp.stack([x[:, 1] for x in first], axis=1), "space", chip_pairs)
    away = attention(
        attend_away, (jnp.stack([other * width, sign]), live, *shared, *first, first_cross, first_chip),
        width, jnp.bfloat16, keys_seen,
    )
    arrived = lax.ppermute(away, "net", swaps(lax.axis_size("net"), 0))
    cross = lax.ppermute(side_by_side(edges), "space", cross_pairs)
    chip = lax.ppermute(side_by_side(inners), "space", chip_pairs)
    kept = attention(
        attend_kept, (jnp.stack([net * width, sign]), live, *shared, *edges, *inners, cross, chip),
        width, jnp.float32, keys_seen,
    )
    return (kept + arrived).astype(jnp.bfloat16)[None]


def solution(mesh):
    return jax.shard_map(
        shards,
        mesh=mesh,
        in_specs=(
            P("net", "tm", "space", None, None),
            P("net", "tm", "space", None, None),
            P("net", "tm", "space", None, None),
            P("net", None, None),
            P("tm", "space", None),
            P("tm", "space"),
            P(),
        ),
        out_specs=P("tm", "space", None, "net"),
        check_vma=False,
    )
```

profile of v0, /device:TPU:11, one launch (start us, length us, event | category | flops | bytes accessed | tf_op | source)
XLA Modules:
  0.0 64.5 jit_solution(2908760425813877810)
XLA Ops:
  0.0 1.5 %dynamic-slice_bitcast_fusion.6 = (bf16[1,64,1280]{2,1,0:T(8,128)(2,1)S(1)}, bf16[1,64,1280]{2,1,0:T(8,128)(2,1)S(1)}, bf16[1,64,1280]{2,1,0:T(8,128)(2,1)S(1)},...) fusion(bf16[1,1,2,64,2560]{4,3,2,1,0:T(8,128)(2,1)} %param.9, ...), kind=kLoop, calls=%fused_computation.19 | loop fusion | bytes 2621456 | tf_op jit(solution)/shard_map/dynamic_slice | solution.py:124
  1.5 0.8 %pad_maximum_fusion.7 = bf16[2,64,1280]{2,1,0:T(8,128)(2,1)} fusion(bf16[1,64,1280]{2,1,0:T(8,128)(2,1)S(1)} %get-tuple-element.15, bf16[1,64,1280]{2,1,0:T(8,128)(2,1)S(1)} %get-tuple-element.24), kind=kLoop, calls=%fused_computation.9 | loop fusion | flops 163840 | bytes 655360 | tf_op jit(solution)/shard_map/stack | solution.py:123
  2.4 4.3 %collective-permute-start.3 = (bf16[2,64,1280]{2,1,0:T(8,128)(2,1)}, bf16[2,64,1280]{2,1,0:T(8,128)(2,1)S(1)}, u32[]{:S(2)}, u32[]{:S(2)}) collective-permute-start(bf16[2,64,1280]{2,1,0:T(8,128)(2,1)} %pad_maximum_fusion.7), channel_id=1, source_target_pairs={{8,16},{16,8},{9,17},{17,9},{10,18},{18,10},{11,19},{19,11},{12,20... | collective-permute-start | bytes 983048 | tf_op jit(solution)/shard_map/ppermute | solution.py:136
  6.8 0.9 %pad_maximum_fusion.4 = bf16[2,2,64,1280]{3,2,1,0:T(8,128)(2,1)} fusion(bf16[2,1,64,1280]{3,2,1,0:T(8,128)(2,1)S(1)} %maximum_bitcast_fusion.1, bf16[2,1,64,1280]{3,2,1,0:T(8,128)(2,1)S(1)} %maximum_bitcast_fusion), kind=kLoop, calls=%fused_computation.4 | loop fusion | flops 327680 | bytes 1310720 | tf_op jit(solution)/shard_map/stack | solution.py:131
  7.8 1.9 %collective-permute-start.9 = (bf16[2,2,64,1280]{3,2,1,0:T(8,128)(2,1)}, bf16[2,2,64,1280]{3,2,1,0:T(8,128)(2,1)S(1)}, u32[]{:S(2)}, u32[]{:S(2)}) collective-permute-start(bf16[2,2,64,1280]{3,2,1,0:T(8,128)(2,1)} %pad_maximum_fusion.4), channel_id=1, source_target_pairs={{8,16},{16,8},{9,17},{17,9},{10,18},{18,10},{11,19},{19,11},{12,20... | collective-permute-start | bytes 1966088 | tf_op jit(solution)/shard_map/ppermute | solution.py:132
  9.7 0.8 %pad_maximum_fusion.8 = bf16[2,64,1280]{2,1,0:T(8,128)(2,1)} fusion(bf16[1,64,1280]{2,1,0:T(8,128)(2,1)S(1)} %get-tuple-element.14, bf16[1,64,1280]{2,1,0:T(8,128)(2,1)S(1)} %get-tuple-element.25), kind=kLoop, calls=%fused_computation.10 | loop fusion | flops 163840 | bytes 655360 | tf_op jit(solution)/shard_map/stack | solution.py:123
  10.5 0.2 collective-permute-start.4
  10.7 1.1 %dynamic-slice_bitcast_fusion = (bf16[1,64,2560]{2,1,0:T(8,128)(2,1)}, bf16[1,64,2560]{2,1,0:T(8,128)(2,1)}, bf16[1,64,2560]{2,1,0:T(8,128)(2,1)}, bf16[1,64,2560]{2,1,0:T(8,128)(2,1)}) fusion(bf16[1,1,2,64,2560]{4,3,2,1,0:T(8,128)(2,1)S(1)} %copy-done.1, s32[]{:T(128)S(6)} %select_n.58, s32[]{:T(128)S(6)} %select_n.57, ...), kind=kLoop, calls=%fused_computation.13 | loop fusion | bytes 2621448 | tf_op jit(solution)/shard_map/jit(dynamic_index_in_dim)/dynamic_slice | solution.py:128
  11.9 2.0 %pad_maximum_fusion = bf16[2,64,2560]{2,1,0:T(8,128)(2,1)} fusion(bf16[1,64,2560]{2,1,0:T(8,128)(2,1)} %get-tuple-element.20, bf16[1,64,2560]{2,1,0:T(8,128)(2,1)} %get-tuple-element.21), kind=kLoop, calls=%fused_computation | loop fusion | flops 327680 | bytes 1310720 | tf_op jit(solution)/shard_map/stack | solution.py:128
  14.1 2.0 %pad_maximum_fusion.1 = bf16[2,64,2560]{2,1,0:T(8,128)(2,1)} fusion(bf16[1,64,2560]{2,1,0:T(8,128)(2,1)} %get-tuple-element.19, bf16[1,64,2560]{2,1,0:T(8,128)(2,1)} %get-tuple-element.22), kind=kLoop, calls=%fused_computation.1 | loop fusion | flops 327680 | bytes 1310720 | tf_op jit(solution)/shard_map/stack | solution.py:128
  16.0 0.2 compare_reduce_fusion
  17.2 11.1 %collective-permute-done.9.odd = bf16[2,2,64,1280]{3,2,1,0:T(8,128)(2,1)S(1)} collective-permute-done((bf16[2,2,64,1280]{3,2,1,0:T(8,128)(2,1)}, bf16[2,2,64,1280]{3,2,1,0:T(8,128)(2,1)S(1)}, u32[]{:S(2)}, u32[]{:S(2)}) %collective-permute-start.9) | collective-permute-done | bytes 655392 | tf_op jit(solution)/shard_map/ppermute | solution.py:132
  28.2 3.1 %collective-permute-start.5 = (bf16[2,64,1280]{2,1,0:T(8,128)(2,1)}, bf16[2,64,1280]{2,1,0:T(8,128)(2,1)S(1)}, u32[]{:S(2)}, u32[]{:S(2)}) collective-permute-start(bf16[2,64,1280]{2,1,0:T(8,128)(2,1)} %pad_maximum_fusion.8), channel_id=1, source_target_pairs={{8,16},{16,8},{9,17},{17,9},{10,18},{18,10},{11,19},{19,11},{12,20... | collective-permute-start | bytes 983048 | tf_op jit(solution)/shard_map/ppermute | solution.py:137
  31.4 5.0 %collective-permute-start = (bf16[2,64,2560]{2,1,0:T(8,128)(2,1)S(1)}, bf16[2,64,2560]{2,1,0:T(8,128)(2,1)S(1)}, u32[]{:S(2)}, u32[]{:S(2)}) collective-permute-start(bf16[2,64,2560]{2,1,0:T(8,128)(2,1)S(1)} %copy-done.5), channel_id=1, source_target_pairs={{2,4},{4,2},{3,5},{5,3},{10,12},{12,10},{11,13},{13,11},{18,20},{2... | collective-permute-start | bytes 1966088 | tf_op jit(solution)/shard_map/ppermute | solution.py:133
  36.6 0.9 %copy-done.4 = bf16[2,64,2560]{2,1,0:T(8,128)(2,1)S(1)} copy-done((bf16[2,64,2560]{2,1,0:T(8,128)(2,1)S(1)}, bf16[2,64,2560]{2,1,0:T(8,128)(2,1)}, u32[]{:S(2)}) %copy-start.4) | copy-done | bytes 655384
  37.5 1.9 %collective-permute-start.10 = (bf16[2,2,64,1280]{3,2,1,0:T(8,128)(2,1)S(1)}, bf16[2,2,64,1280]{3,2,1,0:T(8,128)(2,1)S(1)}, u32[]{:S(2)}, u32[]{:S(2)}) collective-permute-start(bf16[2,2,64,1280]{3,2,1,0:T(8,128)(2,1)S(1)} %pad_maximum_fusion.5), channel_id=1, source_target_pairs={{2,4},{4,2},{3,5},{5,3},{10,12},{12,10},{11,13},{13,11},{18,20},{2... | collective-permute-start | bytes 1966088 | tf_op jit(solution)/shard_map/ppermute | solution.py:157
  39.7 3.9 %collective-permute-start.6 = (bf16[2,2,64,1280]{3,2,1,0:T(8,128)(2,1)S(1)}, bf16[2,2,64,1280]{3,2,1,0:T(8,128)(2,1)S(1)}, u32[]{:S(2)}, u32[]{:S(2)}) collective-permute-start(bf16[2,2,64,1280]{3,2,1,0:T(8,128)(2,1)S(1)} %pad_maximum_fusion.2), channel_id=1, source_target_pairs={{2,4},{4,2},{3,5},{5,3},{10,12},{12,10},{11,13},{13,11},{18,20},{2... | collective-permute-start | bytes 1966088 | tf_op jit(solution)/shard_map/ppermute | solution.py:164
  43.6 1.0 %pad_maximum_fusion.3 = bf16[2,2,64,1280]{3,2,1,0:T(8,128)(2,1)S(1)} fusion(bf16[2,1,64,1280]{3,2,1,0:T(8,128)(2,1)S(1)} %bitcast.72, bf16[2,1,64,1280]{3,2,1,0:T(8,128)(2,1)} %bitcast.32), kind=kLoop, calls=%fused_computation.3 | loop fusion | flops 327680 | bytes 1310720 | tf_op jit(solution)/shard_map/stack | solution.py:16
  44.9 6.8 %collective-permute-done.10.cross = bf16[2,2,64,1280]{3,2,1,0:T(8,128)(2,1)S(1)} collective-permute-done((bf16[2,2,64,1280]{3,2,1,0:T(8,128)(2,1)S(1)}, bf16[2,2,64,1280]{3,2,1,0:T(8,128)(2,1)S(1)}, u32[]{:S(2)}, u32[]{:S(2)}) %collective-permute-start.10) | collective-permute-done | bytes 655392 | tf_op jit(solution)/shard_map/ppermute | solution.py:157
  51.7 4.6 %shard_map.77 = bf16[2,64,1280]{2,1,0:T(8,128)(2,1)S(1)} custom-call(s32[2]{0:T(128)S(1)} %pad_add_fusion.1.scalars, s32[24]{0:T(128)S(1)} %reshape.594.live, bf16[1,256]{1,0:T(2,128)(2,1)S(1)} %fusion.2.feature, bf16[256,2560]{1,0:T(8,128)(2,1)S(1)} %bitcast.66, bf16[2,64,2560]{2,1,0:T(8,128)(2,1)S(1)} %bitcast.68, bf16[2,64,2560]{2,1,0:T(8,128)(2,1)S(1)} %bitcast.62, ...), custom_call_target="tpu_custom_call" | custom-call | flops 503316480 | bytes 3932160 | tf_op jit(solution)/shard_map/pallas_call | solution.py:78
  56.3 0.3 collective-permute-start.12
  56.7 2.0 %collective-permute-done.6.cross = bf16[2,2,64,1280]{3,2,1,0:T(8,128)(2,1)S(1)} collective-permute-done((bf16[2,2,64,1280]{3,2,1,0:T(8,128)(2,1)S(1)}, bf16[2,2,64,1280]{3,2,1,0:T(8,128)(2,1)S(1)}, u32[]{:S(2)}, u32[]{:S(2)}) %collective-permute-start.6) | collective-permute-done | bytes 655392 | tf_op jit(solution)/shard_map/ppermute | solution.py:164
  58.7 5.0 %shard_map.76 = f32[2,64,1280]{2,1,0:T(8,128)S(1)} custom-call(s32[2]{0:T(128)S(1)} %pad_add_fusion.scalars, s32[24]{0:T(128)S(1)} %reshape.594.live, bf16[1,256]{1,0:T(2,128)(2,1)S(1)} %fusion.2.feature, bf16[256,2560]{1,0:T(8,128)(2,1)S(1)} %bitcast.67, bf16[2,64,2560]{2,1,0:T(8,128)(2,1)S(1)} %bitcast.69, bf16[2,64,2560]{2,1,0:T(8,128)(2,1)S(1)} %bitcast.63, ...), custom_call_target="tpu_custom_call" | custom-call | flops 503316480 | bytes 3932160 | tf_op jit(solution)/shard_map/pallas_call | solution.py:78
  63.7 0.8 %fusion = bf16[1,2,64,1280]{3,2,1,0:T(8,128)(2,1)} fusion(f32[2,64,1280]{2,1,0:T(8,128)S(1)} %shard_map.76, bf16[2,64,1280]{2,1,0:T(8,128)(2,1)S(1)} %collective-permute-done.12), kind=kLoop, calls=%fused_computation.8 | loop fusion | flops 491520 | bytes 1310720 | tf_op jit(solution)/shard_map/broadcast_in_dim | solution.py:170
  (48 shorter events, 1.4 us)
Async XLA Ops:
  2.2 34.4 %collective-permute-start.2 = (bf16[2,64,1280]{2,1,0:T(8,128)(2,1)}, bf16[2,64,1280]{2,1,0:T(8,128)(2,1)S(1)}, u32[]{:S(2)}, u32[]{:S(2)}) collective-permute-start(bf16[2,64,1280]{2,1,0:T(8,128)(2,1)} %pad_maximum_fusion.7), channel_id=1, source_target_pairs={{0,8},{16,24},{8,0},{24,16},{1,9},{17,25},{9,1},{25,17},{2,10},{18... | collective-permute-start | bytes 983048 | tf_op jit(solution)/shard_map/ppermute | solution.py:136
  2.4 35.1 %collective-permute-start.3 = (bf16[2,64,1280]{2,1,0:T(8,128)(2,1)}, bf16[2,64,1280]{2,1,0:T(8,128)(2,1)S(1)}, u32[]{:S(2)}, u32[]{:S(2)}) collective-permute-start(bf16[2,64,1280]{2,1,0:T(8,128)(2,1)} %pad_maximum_fusion.7), channel_id=1, source_target_pairs={{8,16},{16,8},{9,17},{17,9},{10,18},{18,10},{11,19},{19,11},{12,20... | collective-permute-start | bytes 983048 | tf_op jit(solution)/shard_map/ppermute | solution.py:136
  6.8 3.9 %copy-start = (bf16[1,1,2,64,2560]{4,3,2,1,0:T(8,128)(2,1)S(1)}, bf16[1,1,2,64,2560]{4,3,2,1,0:T(8,128)(2,1)}, u32[]{:S(2)}) copy-start(bf16[1,1,2,64,2560]{4,3,2,1,0:T(8,128)(2,1)} %param.8) | copy-start | bytes 1966084
  6.8 3.9 %copy-start.1 = (bf16[1,1,2,64,2560]{4,3,2,1,0:T(8,128)(2,1)S(1)}, bf16[1,1,2,64,2560]{4,3,2,1,0:T(8,128)(2,1)}, u32[]{:S(2)}) copy-start(bf16[1,1,2,64,2560]{4,3,2,1,0:T(8,128)(2,1)} %param.9) | copy-start | bytes 1966084
  7.8 23.6 %collective-permute-start.8 = (bf16[2,2,64,1280]{3,2,1,0:T(8,128)(2,1)}, bf16[2,2,64,1280]{3,2,1,0:T(8,128)(2,1)S(1)}, u32[]{:S(2)}, u32[]{:S(2)}) collective-permute-start(bf16[2,2,64,1280]{3,2,1,0:T(8,128)(2,1)} %pad_maximum_fusion.4), channel_id=1, source_target_pairs={{0,8},{16,24},{8,0},{24,16},{1,9},{17,25},{9,1},{25,17},{2,10},{18... | collective-permute-start | bytes 1966088 | tf_op jit(solution)/shard_map/ppermute | solution.py:132
  7.8 20.4 %collective-permute-start.9 = (bf16[2,2,64,1280]{3,2,1,0:T(8,128)(2,1)}, bf16[2,2,64,1280]{3,2,1,0:T(8,128)(2,1)S(1)}, u32[]{:S(2)}, u32[]{:S(2)}) collective-permute-start(bf16[2,2,64,1280]{3,2,1,0:T(8,128)(2,1)} %pad_maximum_fusion.4), channel_id=1, source_target_pairs={{8,16},{16,8},{9,17},{17,9},{10,18},{18,10},{11,19},{19,11},{12,20... | collective-permute-start | bytes 1966088 | tf_op jit(solution)/shard_map/ppermute | solution.py:132
  10.5 29.0 %collective-permute-start.4 = (bf16[2,64,1280]{2,1,0:T(8,128)(2,1)}, bf16[2,64,1280]{2,1,0:T(8,128)(2,1)}, u32[]{:S(2)}, u32[]{:S(2)}) collective-permute-start(bf16[2,64,1280]{2,1,0:T(8,128)(2,1)} %pad_maximum_fusion.8), channel_id=1, source_target_pairs={{0,8},{16,24},{8,0},{24,16},{1,9},{17,25},{9,1},{25,17},{2,10},{18... | collective-permute-start | bytes 983048 | tf_op jit(solution)/shard_map/ppermute | solution.py:137
  10.7 1.1 %copy-start.6 = (s32[1,2,9]{2,1,0:T(2,128)S(1)}, s32[1,2,9]{2,1,0:T(2,128)}, u32[]{:S(2)}) copy-start(s32[1,2,9]{2,1,0:T(2,128)} %param.11) | copy-start | bytes 220
  10.7 1.1 %copy-start.7 = (s32[1,2]{1,0:T(1,128)S(1)}, s32[1,2]{1,0:T(1,128)}, u32[]{:S(2)}) copy-start(s32[1,2]{1,0:T(1,128)} %param.12) | copy-start | bytes 28
  16.4 14.9 %copy-start.5 = (bf16[2,64,2560]{2,1,0:T(8,128)(2,1)S(1)}, bf16[2,64,2560]{2,1,0:T(8,128)(2,1)}, u32[]{:S(2)}) copy-start(bf16[2,64,2560]{2,1,0:T(8,128)(2,1)} %pad_maximum_fusion) | copy-start | bytes 1966084
  28.2 11.4 %collective-permute-start.5 = (bf16[2,64,1280]{2,1,0:T(8,128)(2,1)}, bf16[2,64,1280]{2,1,0:T(8,128)(2,1)S(1)}, u32[]{:S(2)}, u32[]{:S(2)}) collective-permute-start(bf16[2,64,1280]{2,1,0:T(8,128)(2,1)} %pad_maximum_fusion.8), channel_id=1, source_target_pairs={{8,16},{16,8},{9,17},{17,9},{10,18},{18,10},{11,19},{19,11},{12,20... | collective-permute-start | bytes 983048 | tf_op jit(solution)/shard_map/ppermute | solution.py:137
  31.4 13.3 %collective-permute-start = (bf16[2,64,2560]{2,1,0:T(8,128)(2,1)S(1)}, bf16[2,64,2560]{2,1,0:T(8,128)(2,1)S(1)}, u32[]{:S(2)}, u32[]{:S(2)}) collective-permute-start(bf16[2,64,2560]{2,1,0:T(8,128)(2,1)S(1)} %copy-done.5), channel_id=1, source_target_pairs={{2,4},{4,2},{3,5},{5,3},{10,12},{12,10},{11,13},{13,11},{18,20},{2... | collective-permute-start | bytes 1966088 | tf_op jit(solution)/shard_map/ppermute | solution.py:133
  36.4 1.1 %copy-start.4 = (bf16[2,64,2560]{2,1,0:T(8,128)(2,1)S(1)}, bf16[2,64,2560]{2,1,0:T(8,128)(2,1)}, u32[]{:S(2)}) copy-start(bf16[2,64,2560]{2,1,0:T(8,128)(2,1)} %pad_maximum_fusion.1) | copy-start | bytes 1966084
  37.5 7.3 %collective-permute-start.1 = (bf16[2,64,2560]{2,1,0:T(8,128)(2,1)S(1)}, bf16[2,64,2560]{2,1,0:T(8,128)(2,1)S(1)}, u32[]{:S(2)}, u32[]{:S(2)}) collective-permute-start(bf16[2,64,2560]{2,1,0:T(8,128)(2,1)S(1)} %copy-done.4), channel_id=1, source_target_pairs={{0,2},{4,6},{2,0},{6,4},{1,3},{5,7},{3,1},{7,5},{8,10},{12,14},{10... | collective-permute-start | bytes 1966088 | tf_op jit(solution)/shard_map/ppermute | solution.py:134
  37.5 14.1 %collective-permute-start.10 = (bf16[2,2,64,1280]{3,2,1,0:T(8,128)(2,1)S(1)}, bf16[2,2,64,1280]{3,2,1,0:T(8,128)(2,1)S(1)}, u32[]{:S(2)}, u32[]{:S(2)}) collective-permute-start(bf16[2,2,64,1280]{3,2,1,0:T(8,128)(2,1)S(1)} %pad_maximum_fusion.5), channel_id=1, source_target_pairs={{2,4},{4,2},{3,5},{5,3},{10,12},{12,10},{11,13},{13,11},{18,20},{2... | collective-permute-start | bytes 1966088 | tf_op jit(solution)/shard_map/ppermute | solution.py:157
  39.5 12.2 %collective-permute-start.11 = (bf16[2,2,64,1280]{3,2,1,0:T(8,128)(2,1)S(1)}, bf16[2,2,64,1280]{3,2,1,0:T(8,128)(2,1)S(1)}, u32[]{:S(2)}, u32[]{:S(2)}) collective-permute-start(bf16[2,2,64,1280]{3,2,1,0:T(8,128)(2,1)S(1)} %pad_maximum_fusion.6), channel_id=1, source_target_pairs={{0,2},{4,6},{2,0},{6,4},{1,3},{5,7},{3,1},{7,5},{8,10},{12,14},{10... | collective-permute-start | bytes 1966088 | tf_op jit(solution)/shard_map/ppermute | solution.py:158
  39.6 12.1 %copy-start.2 = (bf16[1,256,2560]{2,1,0:T(8,128)(2,1)S(1)}, bf16[1,256,2560]{2,1,0:T(8,128)(2,1)}, u32[]{:S(2)}) copy-start(bf16[1,256,2560]{2,1,0:T(8,128)(2,1)} %param.10) | copy-start | bytes 3932164
  39.6 12.1 %copy-start.3 = (bf16[1,1,2,64,2560]{4,3,2,1,0:T(8,128)(2,1)S(1)}, bf16[1,1,2,64,2560]{4,3,2,1,0:T(8,128)(2,1)}, u32[]{:S(2)}) copy-start(bf16[1,1,2,64,2560]{4,3,2,1,0:T(8,128)(2,1)} %param.7) | copy-start | bytes 1966084
  39.7 19.0 %collective-permute-start.6 = (bf16[2,2,64,1280]{3,2,1,0:T(8,128)(2,1)S(1)}, bf16[2,2,64,1280]{3,2,1,0:T(8,128)(2,1)S(1)}, u32[]{:S(2)}, u32[]{:S(2)}) collective-permute-start(bf16[2,2,64,1280]{3,2,1,0:T(8,128)(2,1)S(1)} %pad_maximum_fusion.2), channel_id=1, source_target_pairs={{2,4},{4,2},{3,5},{5,3},{10,12},{12,10},{11,13},{13,11},{18,20},{2... | collective-permute-start | bytes 1966088 | tf_op jit(solution)/shard_map/ppermute | solution.py:164
  44.7 14.0 %collective-permute-start.7 = (bf16[2,2,64,1280]{3,2,1,0:T(8,128)(2,1)S(1)}, bf16[2,2,64,1280]{3,2,1,0:T(8,128)(2,1)S(1)}, u32[]{:S(2)}, u32[]{:S(2)}) collective-permute-start(bf16[2,2,64,1280]{3,2,1,0:T(8,128)(2,1)S(1)} %pad_maximum_fusion.3), channel_id=1, source_target_pairs={{0,2},{4,6},{2,0},{6,4},{1,3},{5,7},{3,1},{7,5},{8,10},{12,14},{10... | collective-permute-start | bytes 1966088 | tf_op jit(solution)/shard_map/ppermute | solution.py:165
  56.3 7.5 %collective-permute-start.12 = (bf16[2,64,1280]{2,1,0:T(8,128)(2,1)S(1)}, bf16[2,64,1280]{2,1,0:T(8,128)(2,1)S(1)}, u32[]{:S(2)}, u32[]{:S(2)}) collective-permute-start(bf16[2,64,1280]{2,1,0:T(8,128)(2,1)S(1)} %shard_map.77), channel_id=1, source_target_pairs={{0,1},{1,0},{2,3},{3,2},{4,5},{5,4},{6,7},{7,6},{8,9},{9,8},{10,11... | collective-permute-start | bytes 983048 | tf_op jit(solution)/shard_map/ppermute | solution.py:163
where the time goes:
time: 65 us; the launch traced here: 64.5 us
  starting transfers between devices  21 us (32%)
  waiting for transfers between devices  19.9 us (31%)
  Pallas kernels  9.63 us (15%)
  other arithmetic  8.99 us (14%)
  local copies, waits for them, and re-layouts  3.98 us (6%)
  between operations  1 us (2%)
    ppermute x2, waiting for transfers between devices, shards(): first = [lax.ppermute(sent, 'tm', time_pairs[turn]) for turn in time_pairs]  11.1 us
    pallas_call x2, Pallas kernels, attention(): pl.pallas_call(kernel, out_shape=jax.ShapeDtypeStruct((blocks, block_len,...  9.63 us
    ppermute x1, waiting for transfers between devices, shards(): lax.ppermute(jnp.stack([x[:, 0] for x in first], axis=1), 'space', cross_...  6.78 us
    ppermute x1, starting transfers between devices, shards(): own_cross = lax.ppermute(whole(odd), 'space', cross_pairs)  5.02 us
    ppermute x2, starting transfers between devices, shards(): lax.ppermute(edge_sent, 'tm', time_pairs[turn])  4.49 us
    another operation x2, other arithmetic, whole(): jnp.stack([lax.dynamic_index_in_dim(x, which, 0, keepdims=False) for x in...  3.97 us
    ppermute x1, starting transfers between devices, shards(): cross = lax.ppermute(side_by_side(edges), 'space', cross_pairs)  3.93 us
    ppermute x2, starting transfers between devices, shards(): lax.ppermute(inner_sent, 'tm', time_pairs[turn])  3.32 us
  transfers between devices with their start and end apart: 13, of which 3 were waited for; matrix products, arithmetic and copies ran while one was open for 14% of the time, Pallas kernels for 15%

commit v1 on v0

v1 whole, which is shorter than its diff:
```python
import jax
import jax.numpy as jnp
from jax import lax
from jax.experimental import pallas as pl
from jax.experimental.pallas import tpu as pltpu
from jax.sharding import PartitionSpec as P


HD = 128
FREQ = 256
DEAD = -1e30
LOG2E = 1.4426950408889634
VMEM_LIMIT = 6 << 20
SMALL_LIMIT = 2 << 20


def swaps(count, first):
    pairs = [(i, i + 1) for i in range(first, count - 1, 2)]
    return pairs + [(b, a) for a, b in pairs]


def kernel_call(kernel, specs, out_shape, operands, **more):
    return pl.pallas_call(
        kernel, out_shape=out_shape, in_specs=specs,
        out_specs=jax.tree.map(lambda _: pl.BlockSpec(memory_space=pltpu.VMEM), out_shape),
        **more,
    )(*operands)


def on_chip(*arrays):
    return [pltpu.with_memory_space_constraint(x, pltpu.VMEM) for x in arrays]


def pack(at, keys, values, pieces):
    block_len = keys.shape[1]

    def kernel(at_ref, k_ref, v_ref, *rest):
        outs, sems = rest[:len(pieces)], rest[len(pieces)]
        copies = []
        for n, (block, first, width) in enumerate(pieces):
            start = 0 if first is None else pl.multiple_of(at_ref[first], HD)
            for side, source in enumerate((k_ref, v_ref)):
                copies.append(pltpu.make_async_copy(
                    source.at[at_ref[block], :, pl.ds(start, width)], outs[n].at[side], sems.at[n, side]
                ))
        for copy in copies:
            copy.start()
        for copy in copies:
            copy.wait()

    anywhere = pl.BlockSpec(memory_space=pltpu.HBM)
    return kernel_call(
        kernel, [pl.BlockSpec(memory_space=pltpu.SMEM), anywhere, anywhere],
        [jax.ShapeDtypeStruct((2, block_len, width), keys.dtype) for _, _, width in pieces],
        (at, keys, values),
        scratch_shapes=[pltpu.SemaphoreType.DMA((len(pieces), 2))],
        compiler_params=pltpu.CompilerParams(vmem_limit_bytes=SMALL_LIMIT),
    )


def join(even, odd):
    def kernel(even_ref, odd_ref, out_ref):
        out_ref[0] = even_ref[...]
        out_ref[1] = odd_ref[...]

    vmem = pl.BlockSpec(memory_space=pltpu.VMEM)
    return kernel_call(
        kernel, [vmem, vmem], jax.ShapeDtypeStruct((2, *even.shape), even.dtype), on_chip(even, odd),
        compiler_params=pltpu.CompilerParams(vmem_limit_bytes=SMALL_LIMIT),
    )


def time_feature(timestep):
    half = FREQ // 2
    freqs = jnp.exp(-jnp.log(jnp.float32(10000.0)) * jnp.arange(half, dtype=jnp.float32) / half)
    angle = timestep[0].astype(jnp.float32) * freqs
    return jax.nn.silu(jnp.concatenate([jnp.cos(angle), jnp.sin(angle)])).astype(jnp.bfloat16)[None, :]


def signed_gate(feature, proj, sign):
    def kernel(sign_ref, feature_ref, proj_ref, out_ref):
        rows = jnp.broadcast_to(feature_ref[...], (16, feature_ref.shape[-1]))
        gate = jnp.dot(rows, proj_ref[...], preferred_element_type=jnp.float32)
        out_ref[...] = gate[0:1] * sign_ref[0].astype(jnp.float32)

    vmem = pl.BlockSpec(memory_space=pltpu.VMEM)
    return kernel_call(
        kernel, [pl.BlockSpec(memory_space=pltpu.SMEM), vmem, vmem],
        jax.ShapeDtypeStruct((1, proj.shape[-1]), jnp.float32), (sign, feature, proj),
        compiler_params=pltpu.CompilerParams(vmem_limit_bytes=SMALL_LIMIT),
    )


def attend(first_ref, live_ref, gate_ref, q_ref, k_ref, v_ref, own_cross_ref, own_chip_ref,
           even_edge_ref, odd_edge_ref, even_inner_ref, odd_inner_ref, cross_ref, chip_ref, out_ref):
    heads = out_ref.shape[-1] // HD
    block_len = q_ref.shape[1]
    base = first_ref[0]
    near = ((even_edge_ref, even_inner_ref), (odd_edge_ref, odd_inner_ref))
    lane = lax.broadcasted_iota(jnp.int32, (1, 2 * block_len), 1)
    dead = [
        jnp.where(jnp.where(lane < block_len, live_ref[2 * at], live_ref[2 * at + 1]) > 0, 0.0, DEAD)
        for at in range(4 * (1 + len(near)))
    ]

    def at_head(head):
        return slice(head * HD, (head + 1) * HD), pl.ds(pl.multiple_of(base + head * HD, HD), HD)

    def rows(head, side, own_ref):
        here, there = at_head(head)
        parts = [own_ref[0, :, there], own_ref[1, :, there],
                 own_cross_ref[side, :, there], own_chip_ref[side, :, there]]
        for at, (edge_ref, inner_ref) in enumerate(near):
            parts += [edge_ref[side, :, here], inner_ref[side, :, here],
                      cross_ref[at, side, :, here], chip_ref[at, side, :, here]]
        return jnp.concatenate(parts, axis=0)

    def score(head):
        _, there = at_head(head)
        queries = jnp.concatenate([q_ref[0, :, there], q_ref[1, :, there]], axis=0)
        return lax.dot_general(
            rows(head, 0, k_ref), queries, (((1,), (1,)), ((), ())), preferred_element_type=jnp.float32
        )

    scores = score(0)
    for head in range(heads):
        here, there = at_head(head)
        later = score(head + 1) if head + 1 < heads else None
        scores = scores * (HD ** (-0.5) * LOG2E)
        scores = jnp.concatenate(
            [scores[at * block_len:(at + 1) * block_len] + row for at, row in enumerate(dead)], axis=0
        )
        expo = jnp.exp2(scores - jnp.max(scores, axis=0, keepdims=True))
        total = jnp.sum(expo, axis=0, keepdims=True)
        mixed = lax.dot_general(
            expo.astype(jnp.bfloat16), rows(head, 1, v_ref), (((0,), (0,)), ((), ())),
            preferred_element_type=jnp.float32,
        )
        total = jnp.transpose(jnp.broadcast_to(total, (8, 2 * block_len)))[:, 0:1]
        mixed = mixed / total * gate_ref[0:1, there]
        out_ref[0, :, here] = mixed[:block_len].astype(out_ref.dtype)
        out_ref[1, :, here] = mixed[block_len:].astype(out_ref.dtype)
        scores = later


def attention(first, live, operands, width, dtype):
    queries = operands[1]
    blocks, block_len, _ = queries.shape
    keys_seen = live.shape[0] // blocks * block_len
    vmem, smem = (pl.BlockSpec(memory_space=space) for space in (pltpu.VMEM, pltpu.SMEM))
    return kernel_call(
        attend, [smem, smem] + [vmem] * len(operands),
        jax.ShapeDtypeStruct((blocks, block_len, width), dtype),
        (first, live, *on_chip(*operands)),
        cost_estimate=pl.CostEstimate(
            flops=4 * blocks * block_len * keys_seen * width,
            bytes_accessed=4 * keys_seen * width,
            transcendentals=blocks * block_len * keys_seen * width // HD,
        ),
        compiler_params=pltpu.CompilerParams(vmem_limit_bytes=VMEM_LIMIT),
    )


def shards(query_rows, key_rows, value_rows, time_proj, block_list, block_count, timestep):
    queries, keys, values = query_rows[0, 0], key_rows[0, 0], value_rows[0, 0]
    blocks_here, _, features = queries.shape
    assert query_rows.shape[1] == 1 and blocks_here == 2
    width = features // lax.axis_size("net")
    frame, space, net = lax.axis_index("tm"), lax.axis_index("space"), lax.axis_index("net")
    frames, total_blocks = lax.axis_size("tm"), blocks_here * lax.axis_size("space")
    odd = space % 2
    time_pairs = (swaps(frames, 0), swaps(frames, 1))
    chip_pairs, cross_pairs = (swaps(lax.axis_size("space"), first) for first in (0, 1))
    away, kept = (1 - net) * width, net * width
    at = jnp.stack([odd, 1 - odd, away, kept])

    edge_away, inner_away = pack(at, keys, values, [(0, 2, width), (1, 2, width)])
    first_edge = [lax.ppermute(edge_away, "tm", pairs) for pairs in time_pairs]
    first_inner = [lax.ppermute(inner_away, "tm", pairs) for pairs in time_pairs]
    edge_own, inner_own, edge_kept, inner_kept = pack(
        at, keys, values, [(0, None, features), (1, None, features), (0, 3, width), (1, 3, width)]
    )
    own_cross = lax.ppermute(edge_own, "space", cross_pairs)
    own_chip = lax.ppermute(inner_own, "space", chip_pairs)
    kept_edge = [lax.ppermute(edge_kept, "tm", pairs) for pairs in time_pairs]
    kept_inner = [lax.ppermute(inner_kept, "tm", pairs) for pairs in time_pairs]

    step = 1 - 2 * (frame % 2)
    side = 2 * odd - 1
    edge_at, inner_at = 2 * space + odd, 2 * space + 1 - odd
    cross_at, chip_at = edge_at + side, inner_at - side
    at_block = jnp.stack([2 * space, 2 * space + 1, cross_at, chip_at] + [edge_at, inner_at, cross_at, chip_at] * 2)
    at_frame = jnp.stack([frame] * 4 + [frame + step] * 4 + [frame - step] * 4)
    inside = (at_frame >= 0) & (at_frame < frames) & (at_block >= 0) & (at_block < total_blocks)
    name = jnp.where(inside, at_frame * total_blocks + at_block, -1)
    listed = block_list.reshape(blocks_here, -1)
    slots = jnp.arange(listed.shape[-1], dtype=jnp.int32)
    listed = jnp.where(slots[None, :] < block_count.reshape(blocks_here, 1), listed, -2)
    live = jnp.any(listed[None, :, :] == name[:, None, None], axis=-1).astype(jnp.int32).reshape(-1)

    gate = signed_gate(time_feature(timestep), time_proj[0], (2 * net - 1)[None])
    shared = (gate, queries, keys, values, own_cross, own_chip)

    first_cross = lax.ppermute(join(*first_edge), "space", cross_pairs)
    first_chip = lax.ppermute(join(*first_inner), "space", chip_pairs)
    sent = attention(
        away[None], live, (*shared, *first_edge, *first_inner, first_cross, first_chip),
        width, jnp.bfloat16,
    )
    arrived = lax.ppermute(sent, "net", swaps(lax.axis_size("net"), 0))
    kept_cross = lax.ppermute(join(*kept_edge), "space", cross_pairs)
    kept_chip = lax.ppermute(join(*kept_inner), "space", chip_pairs)
    here = attention(
        kept[None], live, (*shared, *kept_edge, *kept_inner, kept_cross, kept_chip),
        width, jnp.float32,
    )
    return (here + arrived).astype(jnp.bfloat16)[None]


def solution(mesh):
    return jax.shard_map(
        shards,
        mesh=mesh,
        in_specs=(
            P("net", "tm", "space", None, None),
            P("net", "tm", "space", None, None),
            P("net", "tm", "space", None, None),
            P("net", None, None),
            P("tm", "space", None),
            P("tm", "space"),
            P(),
        ),
        out_specs=P("tm", "space", None, "net"),
        check_vma=False,
    )
```

time: 65 us -> 62.5 us (0.962)
  the two profiles are of different devices: /device:TPU:11 before, /device:TPU:0 now
where the time goes in v1:
time: 62.5 us; the launch traced here: 62 us
  starting transfers between devices  24.2 us (39%)
  Pallas kernels  14.9 us (24%)
  waiting for transfers between devices  13.3 us (21%)
  local copies, waits for them, and re-layouts  7.33 us (12%)
  other arithmetic  1.19 us (2%)
  between operations  1 us (2%)
    pallas_call x9, Pallas kernels, kernel_call(): pl.pallas_call(kernel, out_shape=out_shape, in_specs=specs, out_specs=jax...  14.9 us
    unnamed x40, local copies, waits for them, and re-layouts  6.97 us
    ppermute x2, starting transfers between devices, shards(): kept_inner = [lax.ppermute(inner_kept, 'tm', pairs) for pairs in time_pairs]  5.28 us
    ppermute x2, starting transfers between devices, shards(): lax.ppermute(inner_away, 'tm', pairs)  5.11 us
    ppermute x1, waiting for transfers between devices, shards(): arrived = lax.ppermute(sent, 'net', swaps(lax.axis_size('net'), 0))  4.62 us
    ppermute x2, waiting for transfers between devices, shards(): kept_inner = [lax.ppermute(inner_kept, 'tm', pairs) for pairs in time_pairs]  4.3 us
    ppermute x2, starting transfers between devices, shards(): first_edge = [lax.ppermute(edge_away, 'tm', pairs) for pairs in time_pairs]  3.79 us
    ppermute x2, waiting for transfers between devices, shards(): kept_edge = [lax.ppermute(edge_kept, 'tm', pairs) for pairs in time_pairs]  2.9 us
  transfers between devices with their start and end apart: 15, of which 4 were waited for; matrix products, arithmetic and copies ran while one was open for 1% of the time, Pallas kernels for 23%

profile of v1, /device:TPU:0, one launch (start us, length us, event | category | flops | bytes accessed | tf_op | source)
XLA Modules:
  0.0 62.0 jit_solution(9704190189556232949)
XLA Ops:
  0.1 1.1 %copy-done = bf16[1,1,2,64,2560]{4,3,2,1,0:T(8,128)(2,1)S(1)} copy-done((bf16[1,1,2,64,2560]{4,3,2,1,0:T(8,128)(2,1)S(1)}, bf16[1,1,2,64,2560]{4,3,2,1,0:T(8,128)(2,1)}, u32[]{:S(2)}) %copy-start) | copy-done | bytes 655384
  1.2 1.1 %copy-done.2 = bf16[1,1,2,64,2560]{4,3,2,1,0:T(8,128)(2,1)S(1)} copy-done((bf16[1,1,2,64,2560]{4,3,2,1,0:T(8,128)(2,1)S(1)}, bf16[1,1,2,64,2560]{4,3,2,1,0:T(8,128)(2,1)}, u32[]{:S(2)}) %copy-start.2) | copy-done | bytes 655384
  3.0 3.1 %collective-permute-start.8 = (bf16[2,64,1280]{2,1,0:T(8,128)(2,1)S(1)}, bf16[2,64,1280]{2,1,0:T(8,128)(2,1)S(1)}, u32[]{:S(2)}, u32[]{:S(2)}) collective-permute-start(bf16[2,64,1280]{2,1,0:T(8,128)(2,1)S(1)} %get-tuple-element.15), channel_id=1, source_target_pairs={{0,8},{16,24},{8,0},{24,16},{1,9},{17,25},{9,1},{25,17},{2,10},{18... | collective-permute-start | bytes 983048 | tf_op jit(solution)/shard_map/ppermute | solution.py:178
  6.8 4.4 %collective-permute-start.10 = (bf16[2,64,1280]{2,1,0:T(8,128)(2,1)S(1)}, bf16[2,64,1280]{2,1,0:T(8,128)(2,1)S(1)}, u32[]{:S(2)}, u32[]{:S(2)}) collective-permute-start(bf16[2,64,1280]{2,1,0:T(8,128)(2,1)S(1)} %get-tuple-element.16), channel_id=1, source_target_pairs={{0,8},{16,24},{8,0},{24,16},{1,9},{17,25},{9,1},{25,17},{2,10},{18... | collective-permute-start | bytes 983048 | tf_op jit(solution)/shard_map/ppermute | solution.py:179
  11.9 2.4 %shard_map.77 = (bf16[2,64,2560]{2,1,0:T(8,128)(2,1)}, bf16[2,64,2560]{2,1,0:T(8,128)(2,1)}, bf16[2,64,1280]{2,1,0:T(8,128)(2,1)}, bf16[2,64,1280]{2,1,0:T(8,128)(2,1)}) custom-call(s32[4]{0:T(128)S(1)} %pad_add_fusion.at_ref, bf16[2,64,2560]{2,1,0:T(8,128)(2,1)S(1)} %bitcast.29, bf16[2,64,2560]{2,1,0:T(8,128)(2,1)S(1)} %bitcast.33), custom_call_target="tpu_custom_call" | custom-call | tf_op jit(solution)/shard_map/pallas_call | solution.py:23
  14.3 1.3 %collective-permute-start.2 = (bf16[2,64,1280]{2,1,0:T(8,128)(2,1)}, bf16[2,64,1280]{2,1,0:T(8,128)(2,1)S(1)}, u32[]{:S(2)}, u32[]{:S(2)}) collective-permute-start(bf16[2,64,1280]{2,1,0:T(8,128)(2,1)} %get-tuple-element.13), channel_id=1, source_target_pairs={{0,8},{16,24},{8,0},{24,16},{1,9},{17,25},{9,1},{25,17},{2,10},{18... | collective-permute-start | bytes 983048 | tf_op jit(solution)/shard_map/ppermute | solution.py:185
  16.3 3.9 %collective-permute-start.4 = (bf16[2,64,1280]{2,1,0:T(8,128)(2,1)}, bf16[2,64,1280]{2,1,0:T(8,128)(2,1)}, u32[]{:S(2)}, u32[]{:S(2)}) collective-permute-start(bf16[2,64,1280]{2,1,0:T(8,128)(2,1)} %get-tuple-element.14), channel_id=1, source_target_pairs={{0,8},{16,24},{8,0},{24,16},{1,9},{17,25},{9,1},{25,17},{2,10},{18... | collective-permute-start | bytes 983048 | tf_op jit(solution)/shard_map/ppermute | solution.py:186
  20.2 1.4 %collective-permute-done.10.even_ref.even_inner_ref = bf16[2,64,1280]{2,1,0:T(8,128)(2,1)S(1)} collective-permute-done((bf16[2,64,1280]{2,1,0:T(8,128)(2,1)S(1)}, bf16[2,64,1280]{2,1,0:T(8,128)(2,1)S(1)}, u32[]{:S(2)}, u32[]{:S(2)}) %collective-permute-start.10) | collective-permute-done | bytes 327712 | tf_op jit(solution)/shard_map/ppermute | solution.py:179
  22.6 0.9 %shard_map.82 = bf16[2,2,64,1280]{3,2,1,0:T(8,128)(2,1)} custom-call(bf16[2,64,1280]{2,1,0:T(8,128)(2,1)S(1)} %collective-permute-done.8.even_ref.even_edge_ref, bf16[2,64,1280]{2,1,0:T(8,128)(2,1)S(1)} %collective-permute-done.9.odd_ref.odd_edge_ref), custom_call_target="tpu_custom_call" | custom-call | tf_op jit(solution)/shard_map/pallas_call | solution.py:23
  23.5 1.4 %collective-permute-start.5 = (bf16[2,64,1280]{2,1,0:T(8,128)(2,1)}, bf16[2,64,1280]{2,1,0:T(8,128)(2,1)}, u32[]{:S(2)}, u32[]{:S(2)}) collective-permute-start(bf16[2,64,1280]{2,1,0:T(8,128)(2,1)} %get-tuple-element.14), channel_id=1, source_target_pairs={{8,16},{16,8},{9,17},{17,9},{10,18},{18,10},{11,19},{19,11},{12,20... | collective-permute-start | bytes 983048 | tf_op jit(solution)/shard_map/ppermute | solution.py:186
  25.8 2.9 %collective-permute-done.2.even_ref.even_edge_ref = bf16[2,64,1280]{2,1,0:T(8,128)(2,1)S(1)} collective-permute-done((bf16[2,64,1280]{2,1,0:T(8,128)(2,1)}, bf16[2,64,1280]{2,1,0:T(8,128)(2,1)S(1)}, u32[]{:S(2)}, u32[]{:S(2)}) %collective-permute-start.2) | collective-permute-done | bytes 327712 | tf_op jit(solution)/shard_map/ppermute | solution.py:185
  29.1 1.5 %collective-permute-start.12 = (bf16[2,2,64,1280]{3,2,1,0:T(8,128)(2,1)}, bf16[2,2,64,1280]{3,2,1,0:T(8,128)(2,1)}, u32[]{:S(2)}, u32[]{:S(2)}) collective-permute-start(bf16[2,2,64,1280]{3,2,1,0:T(8,128)(2,1)} %shard_map.82), channel_id=1, source_target_pairs={{2,4},{4,2},{3,5},{5,3},{10,12},{12,10},{11,13},{13,11},{18,20},{2... | collective-permute-start | bytes 1966088 | tf_op jit(solution)/shard_map/ppermute | solution.py:204
  30.7 4.3 %collective-permute-done.4.even_ref.even_inner_ref = bf16[2,64,1280]{2,1,0:T(8,128)(2,1)} collective-permute-done((bf16[2,64,1280]{2,1,0:T(8,128)(2,1)}, bf16[2,64,1280]{2,1,0:T(8,128)(2,1)}, u32[]{:S(2)}, u32[]{:S(2)}) %collective-permute-start.4) | collective-permute-done | bytes 327712 | tf_op jit(solution)/shard_map/ppermute | solution.py:186
  35.1 0.9 %shard_map.78 = bf16[2,2,64,1280]{3,2,1,0:T(8,128)(2,1)} custom-call(bf16[2,64,1280]{2,1,0:T(8,128)(2,1)S(1)} %collective-permute-done.2.even_ref.even_edge_ref, bf16[2,64,1280]{2,1,0:T(8,128)(2,1)S(1)} %collective-permute-done.3.odd_ref.odd_edge_ref), custom_call_target="tpu_custom_call" | custom-call | tf_op jit(solution)/shard_map/pallas_call | solution.py:23
  37.5 1.6 %collective-permute-start.6 = (bf16[2,2,64,1280]{3,2,1,0:T(8,128)(2,1)}, bf16[2,2,64,1280]{3,2,1,0:T(8,128)(2,1)}, u32[]{:S(2)}, u32[]{:S(2)}) collective-permute-start(bf16[2,2,64,1280]{3,2,1,0:T(8,128)(2,1)} %shard_map.78), channel_id=1, source_target_pairs={{2,4},{4,2},{3,5},{5,3},{10,12},{12,10},{11,13},{13,11},{18,20},{2... | collective-permute-start | bytes 1966088 | tf_op jit(solution)/shard_map/ppermute | solution.py:211
  39.1 2.0 %shard_map.79 = bf16[2,2,64,1280]{3,2,1,0:T(8,128)(2,1)} custom-call(bf16[2,64,1280]{2,1,0:T(8,128)(2,1)} %collective-permute-done.4.even_ref.even_inner_ref, bf16[2,64,1280]{2,1,0:T(8,128)(2,1)} %collective-permute-done.5.odd_ref.odd_inner_ref), custom_call_target="tpu_custom_call" | custom-call | tf_op jit(solution)/shard_map/pallas_call | solution.py:23
  41.0 2.2 %collective-permute-start.7 = (bf16[2,2,64,1280]{3,2,1,0:T(8,128)(2,1)}, bf16[2,2,64,1280]{3,2,1,0:T(8,128)(2,1)}, u32[]{:S(2)}, u32[]{:S(2)}) collective-permute-start(bf16[2,2,64,1280]{3,2,1,0:T(8,128)(2,1)} %shard_map.79), channel_id=1, source_target_pairs={{0,2},{4,6},{2,0},{6,4},{1,3},{5,7},{3,1},{7,5},{8,10},{12,14},{10... | collective-permute-start | bytes 1966088 | tf_op jit(solution)/shard_map/ppermute | solution.py:212
  44.5 1.3 %copy-done.17 = bf16[1,256,2560]{2,1,0:T(8,128)(2,1)S(1)} copy-done((bf16[1,256,2560]{2,1,0:T(8,128)(2,1)S(1)}, bf16[1,256,2560]{2,1,0:T(8,128)(2,1)}, u32[]{:S(2)}) %copy-start.17) | copy-done | bytes 1310744
  46.1 1.0 %copy-done.12 = bf16[2,64,1280]{2,1,0:T(8,128)(2,1)S(1)} copy-done((bf16[2,64,1280]{2,1,0:T(8,128)(2,1)S(1)}, bf16[2,64,1280]{2,1,0:T(8,128)(2,1)}, u32[]{:S(2)}) %copy-start.12) | copy-done | bytes 327704
  47.1 1.0 %copy-done.16 = bf16[2,64,1280]{2,1,0:T(8,128)(2,1)S(1)} copy-done((bf16[2,64,1280]{2,1,0:T(8,128)(2,1)S(1)}, bf16[2,64,1280]{2,1,0:T(8,128)(2,1)}, u32[]{:S(2)}) %copy-start.16) | copy-done | bytes 327704
  48.1 3.4 %shard_map.84 = bf16[2,64,1280]{2,1,0:T(8,128)(2,1)S(1)} custom-call(s32[1]{0:T(128)} %bitcast.22.first_ref, s32[24]{0:T(128)S(1)} %reshape.582.live_ref, f32[1,2560]{1,0:T(1,128)S(1)} %shard_map.76.gate_ref, bf16[2,64,2560]{2,1,0:T(8,128)(2,1)S(1)} %bitcast.36, bf16[2,64,2560]{2,1,0:T(8,128)(2,1)S(1)} %bitcast.30, bf16[2,64,2560]{2,1,0:T(8,128)(2,1)S(1)} %bitcast.34, ...), custom_call_target="tpu_custom_call" | custom-call | flops 503316480 | bytes 3932160 | tf_op jit(solution)/shard_map/pallas_call | solution.py:23
  51.5 1.5 %collective-permute-start.14 = (bf16[2,64,1280]{2,1,0:T(8,128)(2,1)S(1)}, bf16[2,64,1280]{2,1,0:T(8,128)(2,1)S(1)}, u32[]{:S(2)}, u32[]{:S(2)}) collective-permute-start(bf16[2,64,1280]{2,1,0:T(8,128)(2,1)S(1)} %shard_map.84), channel_id=1, source_target_pairs={{0,1},{1,0},{2,3},{3,2},{4,5},{5,4},{6,7},{7,6},{8,9},{9,8},{10,11... | collective-permute-start | bytes 983048 | tf_op jit(solution)/shard_map/ppermute | solution.py:210
  53.1 3.5 %shard_map.80 = f32[2,64,1280]{2,1,0:T(8,128)S(1)} custom-call(s32[1]{0:T(128)} %bitcast.first_ref, s32[24]{0:T(128)S(1)} %reshape.582.live_ref, f32[1,2560]{1,0:T(1,128)S(1)} %shard_map.76.gate_ref, bf16[2,64,2560]{2,1,0:T(8,128)(2,1)S(1)} %bitcast.37, bf16[2,64,2560]{2,1,0:T(8,128)(2,1)S(1)} %bitcast.31, bf16[2,64,2560]{2,1,0:T(8,128)(2,1)S(1)} %bitcast.35, ...), custom_call_target="tpu_custom_call" | custom-call | flops 503316480 | bytes 3932160 | tf_op jit(solution)/shard_map/pallas_call | solution.py:23
  56.6 4.6 %collective-permute-done.14 = bf16[2,64,1280]{2,1,0:T(8,128)(2,1)S(1)} collective-permute-done((bf16[2,64,1280]{2,1,0:T(8,128)(2,1)S(1)}, bf16[2,64,1280]{2,1,0:T(8,128)(2,1)S(1)}, u32[]{:S(2)}, u32[]{:S(2)}) %collective-permute-start.14) | collective-permute-done | bytes 327712 | tf_op jit(solution)/shard_map/ppermute | solution.py:210
  (67 shorter events, 8.2 us)
Async XLA Ops:
  3.0 12.7 %collective-permute-start.8 = (bf16[2,64,1280]{2,1,0:T(8,128)(2,1)S(1)}, bf16[2,64,1280]{2,1,0:T(8,128)(2,1)S(1)}, u32[]{:S(2)}, u32[]{:S(2)}) collective-permute-start(bf16[2,64,1280]{2,1,0:T(8,128)(2,1)S(1)} %get-tuple-element.15), channel_id=1, source_target_pairs={{0,8},{16,24},{8,0},{24,16},{1,9},{17,25},{9,1},{25,17},{2,10},{18... | collective-permute-start | bytes 983048 | tf_op jit(solution)/shard_map/ppermute | solution.py:178
  6.1 10.2 %collective-permute-start.9 = (bf16[2,64,1280]{2,1,0:T(8,128)(2,1)S(1)}, bf16[2,64,1280]{2,1,0:T(8,128)(2,1)S(1)}, u32[]{:S(2)}, u32[]{:S(2)}) collective-permute-start(bf16[2,64,1280]{2,1,0:T(8,128)(2,1)S(1)} %get-tuple-element.15), channel_id=1, source_target_pairs={{8,16},{16,8},{9,17},{17,9},{10,18},{18,10},{11,19},{19,11},{12,20... | collective-permute-start | bytes 983048 | tf_op jit(solution)/shard_map/ppermute | solution.py:178
  6.8 14.9 %collective-permute-start.10 = (bf16[2,64,1280]{2,1,0:T(8,128)(2,1)S(1)}, bf16[2,64,1280]{2,1,0:T(8,128)(2,1)S(1)}, u32[]{:S(2)}, u32[]{:S(2)}) collective-permute-start(bf16[2,64,1280]{2,1,0:T(8,128)(2,1)S(1)} %get-tuple-element.16), channel_id=1, source_target_pairs={{0,8},{16,24},{8,0},{24,16},{1,9},{17,25},{9,1},{25,17},{2,10},{18... | collective-permute-start | bytes 983048 | tf_op jit(solution)/shard_map/ppermute | solution.py:179
  11.2 12.3 %collective-permute-start.11 = (bf16[2,64,1280]{2,1,0:T(8,128)(2,1)S(1)}, bf16[2,64,1280]{2,1,0:T(8,128)(2,1)S(1)}, u32[]{:S(2)}, u32[]{:S(2)}) collective-permute-start(bf16[2,64,1280]{2,1,0:T(8,128)(2,1)S(1)} %get-tuple-element.16), channel_id=1, source_target_pairs={{8,16},{16,8},{9,17},{17,9},{10,18},{18,10},{11,19},{19,11},{12,20... | collective-permute-start | bytes 983048 | tf_op jit(solution)/shard_map/ppermute | solution.py:179
  14.3 14.4 %collective-permute-start.2 = (bf16[2,64,1280]{2,1,0:T(8,128)(2,1)}, bf16[2,64,1280]{2,1,0:T(8,128)(2,1)S(1)}, u32[]{:S(2)}, u32[]{:S(2)}) collective-permute-start(bf16[2,64,1280]{2,1,0:T(8,128)(2,1)} %get-tuple-element.13), channel_id=1, source_target_pairs={{0,8},{16,24},{8,0},{24,16},{1,9},{17,25},{9,1},{25,17},{2,10},{18... | collective-permute-start | bytes 983048 | tf_op jit(solution)/shard_map/ppermute | solution.py:185
  15.6 10.1 %copy-start.5 = (bf16[2,64,1280]{2,1,0:T(8,128)(2,1)}, bf16[2,64,1280]{2,1,0:T(8,128)(2,1)S(1)}, u32[]{:S(2)}) copy-start(bf16[2,64,1280]{2,1,0:T(8,128)(2,1)S(1)} %collective-permute-done.8.even_ref.even_edge_ref) | copy-start | bytes 983044
  15.6 13.5 %collective-permute-start.3 = (bf16[2,64,1280]{2,1,0:T(8,128)(2,1)}, bf16[2,64,1280]{2,1,0:T(8,128)(2,1)S(1)}, u32[]{:S(2)}, u32[]{:S(2)}) collective-permute-start(bf16[2,64,1280]{2,1,0:T(8,128)(2,1)} %get-tuple-element.13), channel_id=1, source_target_pairs={{8,16},{16,8},{9,17},{17,9},{10,18},{18,10},{11,19},{19,11},{12,20... | collective-permute-start | bytes 983048 | tf_op jit(solution)/shard_map/ppermute | solution.py:185
  16.3 9.5 %copy-start.7 = (bf16[2,64,1280]{2,1,0:T(8,128)(2,1)}, bf16[2,64,1280]{2,1,0:T(8,128)(2,1)S(1)}, u32[]{:S(2)}) copy-start(bf16[2,64,1280]{2,1,0:T(8,128)(2,1)S(1)} %collective-permute-done.9.odd_ref.odd_edge_ref) | copy-start | bytes 983044
  16.3 18.6 %collective-permute-start.4 = (bf16[2,64,1280]{2,1,0:T(8,128)(2,1)}, bf16[2,64,1280]{2,1,0:T(8,128)(2,1)}, u32[]{:S(2)}, u32[]{:S(2)}) collective-permute-start(bf16[2,64,1280]{2,1,0:T(8,128)(2,1)} %get-tuple-element.14), channel_id=1, source_target_pairs={{0,8},{16,24},{8,0},{24,16},{1,9},{17,25},{9,1},{25,17},{2,10},{18... | collective-permute-start | bytes 983048 | tf_op jit(solution)/shard_map/ppermute | solution.py:186
  21.7 19.4 %collective-permute-start = (bf16[2,64,2560]{2,1,0:T(8,128)(2,1)}, bf16[2,64,2560]{2,1,0:T(8,128)(2,1)S(1)}, u32[]{:S(2)}, u32[]{:S(2)}) collective-permute-start(bf16[2,64,2560]{2,1,0:T(8,128)(2,1)} %get-tuple-element.11), channel_id=1, source_target_pairs={{2,4},{4,2},{3,5},{5,3},{10,12},{12,10},{11,13},{13,11},{18,20},{2... | collective-permute-start | bytes 1966088 | tf_op jit(solution)/shard_map/ppermute | solution.py:183
  22.6 12.4 %copy-start.18 = (s32[1,2,9]{2,1,0:T(2,128)S(1)}, s32[1,2,9]{2,1,0:T(2,128)}, u32[]{:S(2)}) copy-start(s32[1,2,9]{2,1,0:T(2,128)} %param.11) | copy-start | bytes 220
  22.6 12.4 %copy-start.19 = (s32[1,2]{1,0:T(1,128)S(1)}, s32[1,2]{1,0:T(1,128)}, u32[]{:S(2)}) copy-start(s32[1,2]{1,0:T(1,128)} %param.12) | copy-start | bytes 28
  23.5 11.6 %copy-start.15 = (bf16[2,64,1280]{2,1,0:T(8,128)(2,1)}, bf16[2,64,1280]{2,1,0:T(8,128)(2,1)S(1)}, u32[]{:S(2)}) copy-start(bf16[2,64,1280]{2,1,0:T(8,128)(2,1)S(1)} %collective-permute-done.11.odd_ref.odd_inner_ref) | copy-start | bytes 983044
  23.5 14.0 %collective-permute-start.5 = (bf16[2,64,1280]{2,1,0:T(8,128)(2,1)}, bf16[2,64,1280]{2,1,0:T(8,128)(2,1)}, u32[]{:S(2)}, u32[]{:S(2)}) collective-permute-start(bf16[2,64,1280]{2,1,0:T(8,128)(2,1)} %get-tuple-element.14), channel_id=1, source_target_pairs={{8,16},{16,8},{9,17},{17,9},{10,18},{18,10},{11,19},{19,11},{12,20... | collective-permute-start | bytes 983048 | tf_op jit(solution)/shard_map/ppermute | solution.py:186
  28.7 17.4 %collective-permute-start.1 = (bf16[2,64,2560]{2,1,0:T(8,128)(2,1)}, bf16[2,64,2560]{2,1,0:T(8,128)(2,1)S(1)}, u32[]{:S(2)}, u32[]{:S(2)}) collective-permute-start(bf16[2,64,2560]{2,1,0:T(8,128)(2,1)} %get-tuple-element.12), channel_id=1, source_target_pairs={{0,2},{4,6},{2,0},{6,4},{1,3},{5,7},{3,1},{7,5},{8,10},{12,14},{10... | collective-permute-start | bytes 1966088 | tf_op jit(solution)/shard_map/ppermute | solution.py:184
  29.1 16.9 %collective-permute-start.12 = (bf16[2,2,64,1280]{3,2,1,0:T(8,128)(2,1)}, bf16[2,2,64,1280]{3,2,1,0:T(8,128)(2,1)}, u32[]{:S(2)}, u32[]{:S(2)}) collective-permute-start(bf16[2,2,64,1280]{3,2,1,0:T(8,128)(2,1)} %shard_map.82), channel_id=1, source_target_pairs={{2,4},{4,2},{3,5},{5,3},{10,12},{12,10},{11,13},{13,11},{18,20},{2... | collective-permute-start | bytes 1966088 | tf_op jit(solution)/shard_map/ppermute | solution.py:204
  35.0 11.1 %collective-permute-start.13 = (bf16[2,2,64,1280]{3,2,1,0:T(8,128)(2,1)}, bf16[2,2,64,1280]{3,2,1,0:T(8,128)(2,1)}, u32[]{:S(2)}, u32[]{:S(2)}) collective-permute-start(bf16[2,2,64,1280]{3,2,1,0:T(8,128)(2,1)} %shard_map.83), channel_id=1, source_target_pairs={{0,2},{4,6},{2,0},{6,4},{1,3},{5,7},{3,1},{7,5},{8,10},{12,14},{10... | collective-permute-start | bytes 1966088 | tf_op jit(solution)/shard_map/ppermute | solution.py:205
  37.4 8.6 %copy-start.1 = (bf16[1,1,2,64,2560]{4,3,2,1,0:T(8,128)(2,1)S(1)}, bf16[1,1,2,64,2560]{4,3,2,1,0:T(8,128)(2,1)}, u32[]{:S(2)}) copy-start(bf16[1,1,2,64,2560]{4,3,2,1,0:T(8,128)(2,1)} %param.8) | copy-start | bytes 1966084
  37.5 8.7 %copy-start.3 = (bf16[1,1,2,64,2560]{4,3,2,1,0:T(8,128)(2,1)S(1)}, bf16[1,1,2,64,2560]{4,3,2,1,0:T(8,128)(2,1)}, u32[]{:S(2)}) copy-start(bf16[1,1,2,64,2560]{4,3,2,1,0:T(8,128)(2,1)} %param.9) | copy-start | bytes 1966084
  37.5 8.7 %copy-start.4 = (bf16[1,1,2,64,2560]{4,3,2,1,0:T(8,128)(2,1)S(1)}, bf16[1,1,2,64,2560]{4,3,2,1,0:T(8,128)(2,1)}, u32[]{:S(2)}) copy-start(bf16[1,1,2,64,2560]{4,3,2,1,0:T(8,128)(2,1)} %param.7) | copy-start | bytes 1966084
  37.5 15.6 %collective-permute-start.6 = (bf16[2,2,64,1280]{3,2,1,0:T(8,128)(2,1)}, bf16[2,2,64,1280]{3,2,1,0:T(8,128)(2,1)}, u32[]{:S(2)}, u32[]{:S(2)}) collective-permute-start(bf16[2,2,64,1280]{3,2,1,0:T(8,128)(2,1)} %shard_map.78), channel_id=1, source_target_pairs={{2,4},{4,2},{3,5},{5,3},{10,12},{12,10},{11,13},{13,11},{18,20},{2... | collective-permute-start | bytes 1966088 | tf_op jit(solution)/shard_map/ppermute | solution.py:211
  41.0 12.0 %collective-permute-start.7 = (bf16[2,2,64,1280]{3,2,1,0:T(8,128)(2,1)}, bf16[2,2,64,1280]{3,2,1,0:T(8,128)(2,1)}, u32[]{:S(2)}, u32[]{:S(2)}) collective-permute-start(bf16[2,2,64,1280]{3,2,1,0:T(8,128)(2,1)} %shard_map.79), channel_id=1, source_target_pairs={{0,2},{4,6},{2,0},{6,4},{1,3},{5,7},{3,1},{7,5},{8,10},{12,14},{10... | collective-permute-start | bytes 1966088 | tf_op jit(solution)/shard_map/ppermute | solution.py:212
  48.1 5.0 %copy-start.14 = (bf16[2,64,1280]{2,1,0:T(8,128)(2,1)S(1)}, bf16[2,64,1280]{2,1,0:T(8,128)(2,1)}, u32[]{:S(2)}) copy-start(bf16[2,64,1280]{2,1,0:T(8,128)(2,1)} %copy-done.13) | copy-start | bytes 983044
  51.5 9.7 %collective-permute-start.14 = (bf16[2,64,1280]{2,1,0:T(8,128)(2,1)S(1)}, bf16[2,64,1280]{2,1,0:T(8,128)(2,1)S(1)}, u32[]{:S(2)}, u32[]{:S(2)}) collective-permute-start(bf16[2,64,1280]{2,1,0:T(8,128)(2,1)S(1)} %shard_map.84), channel_id=1, source_target_pairs={{0,1},{1,0},{2,3},{3,2},{4,5},{5,4},{6,7},{7,6},{8,9},{9,8},{10,11... | collective-permute-start | bytes 983048 | tf_op jit(solution)/shard_map/ppermute | solution.py:210
  (11 other events, 21.0 us)

commit v2 on v1

v2 whole, which is shorter than its diff:
```python
import functools

import jax
import jax.numpy as jnp
from jax import lax
from jax.experimental import pallas as pl
from jax.experimental.pallas import tpu as pltpu
from jax.sharding import PartitionSpec as P


HD = 128
FREQ = 256
DEAD = -1e30
LOG2E = 1.4426950408889634
VMEM_LIMIT = 6 << 20
SMALL_LIMIT = 2 << 20


def swaps(count, first):
    pairs = [(i, i + 1) for i in range(first, count - 1, 2)]
    return pairs + [(b, a) for a, b in pairs]


def kernel_call(kernel, specs, out_shape, operands, **more):
    return pl.pallas_call(
        kernel, out_shape=out_shape, in_specs=specs,
        out_specs=(
            [pl.BlockSpec(memory_space=pltpu.VMEM)] * len(out_shape) if isinstance(out_shape, list)
            else pl.BlockSpec(memory_space=pltpu.VMEM)
        ),
        **more,
    )(*operands)


def on_chip(*arrays):
    return [pltpu.with_memory_space_constraint(x, pltpu.VMEM) for x in arrays]


def place():
    odd = lax.rem(lax.axis_index("space"), 2)
    return odd, lax.axis_index("net")


def pack(keys, values, pieces, *gate_of):
    block_len, features = keys.shape[1:]
    half = features // lax.axis_size("net")
    widths = [features if which == "both" else half for _, which in pieces]

    def kernel(k_ref, v_ref, *rest):
        inputs, rest = rest[:len(gate_of)], rest[len(gate_of):]
        outs, rest = rest[:len(pieces)], rest[len(pieces):]
        odd, net = place()
        sems = rest[-1]
        copies = []
        for n, (block, which) in enumerate(pieces):
            row = odd if block == "edge" else 1 - odd
            start = {"both": 0, "kept": net * half, "away": (1 - net) * half}[which]
            if which != "both":
                start = pl.multiple_of(start, HD)
            for side, source in enumerate((k_ref, v_ref)):
                copies.append(pltpu.make_async_copy(
                    source.at[row, :, pl.ds(start, widths[n])], outs[n].at[side], sems.at[n, side]
                ))
        for copy in copies:
            copy.start()
        if gate_of:
            (feature_ref, proj_ref), (gate_ref, held_ref) = inputs, rest[:2]
            fetch = pltpu.make_async_copy(proj_ref, held_ref, sems.at[len(pieces), 0])
            fetch.start()
            fetch.wait()
            rows = jnp.broadcast_to(feature_ref[...], (16, feature_ref.shape[-1]))
            gate = jnp.dot(rows, held_ref[...], preferred_element_type=jnp.float32)
            gate_ref[...] = gate[0:1] * (2 * net - 1).astype(jnp.float32)
        for copy in copies:
            copy.wait()

    hbm, vmem = pl.BlockSpec(memory_space=pltpu.HBM), pl.BlockSpec(memory_space=pltpu.VMEM)
    operands = [pltpu.with_memory_space_constraint(x, pltpu.HBM) for x in (keys, values)]
    out_shape = [jax.ShapeDtypeStruct((2, block_len, width), keys.dtype) for width in widths]
    specs, scratch = [hbm, hbm], []
    if gate_of:
        feature, proj = gate_of
        operands += [feature, pltpu.with_memory_space_constraint(proj, pltpu.HBM)]
        specs += [vmem, hbm]
        out_shape.append(jax.ShapeDtypeStruct((1, features), jnp.float32))
        scratch = [pltpu.VMEM(proj.shape, proj.dtype)]
    return kernel_call(
        kernel, specs, out_shape, operands,
        scratch_shapes=[*scratch, pltpu.SemaphoreType.DMA((len(pieces) + 1, 2))],
        compiler_params=pltpu.CompilerParams(vmem_limit_bytes=VMEM_LIMIT),
    )


def join(odd, even):
    def kernel(even_ref, odd_ref, out_ref):
        out_ref[0] = even_ref[...]
        out_ref[1] = odd_ref[...]

    vmem = pl.BlockSpec(memory_space=pltpu.VMEM)
    return kernel_call(
        kernel, [vmem, vmem], jax.ShapeDtypeStruct((2, *even.shape), even.dtype), on_chip(even, odd),
        compiler_params=pltpu.CompilerParams(vmem_limit_bytes=SMALL_LIMIT),
    )


def time_feature(timestep):
    half = FREQ // 2
    freqs = jnp.exp(-jnp.log(jnp.float32(10000.0)) * jnp.arange(half, dtype=jnp.float32) / half)
    angle = timestep[0].astype(jnp.float32) * freqs
    return jax.nn.silu(jnp.concatenate([jnp.cos(angle), jnp.sin(angle)])).astype(jnp.bfloat16)[None, :]


def dead_rows(list_ref, count_ref, block_len):
    frame, space = lax.axis_index("tm"), lax.axis_index("space")
    frames, total_blocks = lax.axis_size("tm"), 2 * lax.axis_size("space")
    odd = lax.rem(space, 2)
    step, side = 1 - 2 * lax.rem(frame, 2), 2 * odd - 1
    edge_at, inner_at = 2 * space + odd, 2 * space + 1 - odd
    outer = [edge_at + side, inner_at - side]
    lane = lax.broadcasted_iota(jnp.int32, (1, 2 * block_len), 1)
    listed = [
        jnp.where(
            lane < block_len,
            jnp.where(slot < count_ref[0, 0], list_ref[0, slot], -2),
            jnp.where(slot < count_ref[0, 1], list_ref[1, slot], -2),
        )
        for slot in range(list_ref.shape[1])
    ]
    dead = []
    for at_frame, near in (
        (frame, [2 * space, 2 * space + 1]), (frame + step, [edge_at, inner_at]), (frame - step, [edge_at, inner_at]),
    ):
        for at_block in near + outer:
            inside = (at_frame >= 0) & (at_frame < frames) & (at_block >= 0) & (at_block < total_blocks)
            name = jnp.where(inside, at_frame * total_blocks + at_block, -1)
            live = listed[0] == name
            for entry in listed[1:]:
                live = live | (entry == name)
            dead.append(jnp.where(live, 0.0, DEAD))
    return dead


def attend(kept, list_ref, count_ref, gate_ref, q_ref, k_ref, v_ref, own_cross_ref, own_chip_ref,
           odd_edge_ref, even_edge_ref, odd_inner_ref, even_inner_ref, cross_ref, chip_ref, out_ref):
    heads = out_ref.shape[-1] // HD
    block_len = q_ref.shape[1]
    net = lax.axis_index("net")
    base = (net if kept else 1 - net) * out_ref.shape[-1]
    near = ((even_edge_ref, even_inner_ref), (odd_edge_ref, odd_inner_ref))
    dead = dead_rows(list_ref, count_ref, block_len)

    def at_head(head):
        return slice(head * HD, (head + 1) * HD), pl.ds(pl.multiple_of(base + head * HD, HD), HD)

    def rows(head, side, own_ref):
        here, there = at_head(head)
        parts = [own_ref[0, :, there], own_ref[1, :, there],
                 own_cross_ref[side, :, there], own_chip_ref[side, :, there]]
        for at, (edge_ref, inner_ref) in enumerate(near):
            parts += [edge_ref[side, :, here], inner_ref[side, :, here],
                      cross_ref[at, side, :, here], chip_ref[at, side, :, here]]
        return jnp.concatenate(parts, axis=0)

    def score(head):
        _, there = at_head(head)
        queries = jnp.concatenate([q_ref[0, :, there], q_ref[1, :, there]], axis=0)
        return lax.dot_general(
            rows(head, 0, k_ref), queries, (((1,), (1,)), ((), ())), preferred_element_type=jnp.float32
        )

    scores = score(0)
    for head in range(heads):
        here, there = at_head(head)
        later = score(head + 1) if head + 1 < heads else None
        scores = scores * (HD ** (-0.5) * LOG2E)
        scores = jnp.concatenate(
            [scores[at * block_len:(at + 1) * block_len] + row for at, row in enumerate(dead)], axis=0
        )
        expo = jnp.exp2(scores - jnp.max(scores, axis=0, keepdims=True))
        total = jnp.sum(expo, axis=0, keepdims=True)
        mixed = lax.dot_general(
            expo.astype(jnp.bfloat16), rows(head, 1, v_ref), (((0,), (0,)), ((), ())),
            preferred_element_type=jnp.float32,
        )
        total = jnp.transpose(jnp.broadcast_to(total, (8, 2 * block_len)))[:, 0:1]
        mixed = mixed / total * gate_ref[0:1, there]
        out_ref[0, :, here] = mixed[:block_len].astype(out_ref.dtype)
        out_ref[1, :, here] = mixed[block_len:].astype(out_ref.dtype)
        scores = later


def attention(kept, listed, count, operands, width, dtype):
    queries = operands[1]
    blocks, block_len, _ = queries.shape
    keys_seen = 12 * block_len
    vmem, smem = (pl.BlockSpec(memory_space=space) for space in (pltpu.VMEM, pltpu.SMEM))
    return kernel_call(
        functools.partial(attend, kept), [smem, smem] + [vmem] * len(operands),
        jax.ShapeDtypeStruct((blocks, block_len, width), dtype),
        (listed, count, *on_chip(*operands)),
        cost_estimate=pl.CostEstimate(
            flops=4 * blocks * block_len * keys_seen * width,
            bytes_accessed=4 * keys_seen * width,
            transcendentals=blocks * block_len * keys_seen * width // HD,
        ),
        compiler_params=pltpu.CompilerParams(vmem_limit_bytes=VMEM_LIMIT),
    )


def shards(query_rows, key_rows, value_rows, time_proj, block_list, block_count, timestep):
    queries, keys, values = query_rows[0, 0], key_rows[0, 0], value_rows[0, 0]
    blocks_here, _, features = queries.shape
    assert query_rows.shape[1] == 1 and blocks_here == 2
    width = features // lax.axis_size("net")
    time_pairs = (swaps(lax.axis_size("tm"), 1), swaps(lax.axis_size("tm"), 0))
    chip_pairs, cross_pairs = (swaps(lax.axis_size("space"), first) for first in (0, 1))

    edge_away, inner_away = pack(keys, values, [("edge", "away"), ("inner", "away")])
    first_edge = [lax.ppermute(edge_away, "tm", pairs) for pairs in time_pairs]
    first_inner = [lax.ppermute(inner_away, "tm", pairs) for pairs in time_pairs]
    edge_own, inner_own, edge_kept, inner_kept, gate = pack(
        keys, values, [("edge", "both"), ("inner", "both"), ("edge", "kept"), ("inner", "kept")],
        time_feature(timestep), time_proj[0],
    )
    own_cross = lax.ppermute(edge_own, "space", cross_pairs)
    own_chip = lax.ppermute(inner_own, "space", chip_pairs)
    kept_edge = [lax.ppermute(edge_kept, "tm", pairs) for pairs in time_pairs]
    kept_inner = [lax.ppermute(inner_kept, "tm", pairs) for pairs in time_pairs]

    listed = (block_list[0], block_count)
    shared = (gate, queries, keys, values, own_cross, own_chip)

    first_cross = lax.ppermute(join(*first_edge), "space", cross_pairs)
    first_chip = lax.ppermute(join(*first_inner), "space", chip_pairs)
    sent = attention(
        False, *listed, (*shared, *first_edge, *first_inner, first_cross, first_chip),
        width, jnp.bfloat16,
    )
    arrived = lax.ppermute(sent, "net", swaps(lax.axis_size("net"), 0))
    kept_cross = lax.ppermute(join(*kept_edge), "space", cross_pairs)
    kept_chip = lax.ppermute(join(*kept_inner), "space", chip_pairs)
    here = attention(
        True, *listed, (*shared, *kept_edge, *kept_inner, kept_cross, kept_chip),
        width, jnp.float32,
    )
    return (here + arrived).astype(jnp.bfloat16)[None]


def solution(mesh):
    return jax.shard_map(
        shards,
        mesh=mesh,
        in_specs=(
            P("net", "tm", "space", None, None),
            P("net", "tm", "space", None, None),
            P("net", "tm", "space", None, None),
            P("net", None, None),
            P("tm", "space", None),
            P("tm", "space"),
            P(),
        ),
        out_specs=P("tm", "space", None, "net"),
        check_vma=False,
    )
```

time: 62.5 us -> 60.7 us (0.971)
  waiting for transfers between devices: 13.3 us -> 22.3 us
  local copies, waits for them, and re-layouts: 7.33 us -> 0.03 us
  Pallas kernels: 14.9 us -> 8.99 us
  starting transfers between devices: 24.2 us -> 27.3 us
    unnamed x40 -> x10, local copies, waits for them, and re-layouts: 6.97 us -> 0.03 us
    pallas_call x9 -> x8, Pallas kernels: 14.9 us -> 8.99 us  [kernel_call(): pl.pallas_call(kernel, out_shape=out_shape, in_specs=specs, out_specs=[pl...]
    ppermute x2, waiting for transfers between devices: 1.44 us -> 5.04 us  [shards(): lax.ppermute(inner_away, 'tm', pairs)]
    ppermute x2, starting transfers between devices: 3.79 us -> 6.6 us  [shards(): first_edge = [lax.ppermute(edge_away, 'tm', pairs) for pairs in time_pairs]]
    ppermute x2, starting transfers between devices: 5.28 us -> 8.04 us  [shards(): kept_inner = [lax.ppermute(inner_kept, 'tm', pairs) for pairs in time_pairs]]
    ppermute x2, starting transfers between devices: 5.11 us -> 2.44 us  [shards(): lax.ppermute(inner_away, 'tm', pairs)]
    ppermute x2, waiting for transfers between devices: 4.3 us -> 6.81 us  [shards(): kept_inner = [lax.ppermute(inner_kept, 'tm', pairs) for pairs in time_pairs]]
    ppermute x2, waiting for transfers between devices: 2.9 us -> 4.93 us  [shards(): kept_edge = [lax.ppermute(edge_kept, 'tm', pairs) for pairs in time_pairs]]
  transfers between devices with their start and end apart: 15 -> 15, of which waited for: 4 -> 4; matrix products, arithmetic and copies ran while one was open for 1% -> 0% of each run, Pallas kernels for 23% -> 13%
where the time goes in v2:
time: 60.7 us; the launch traced here: 60.4 us
  starting transfers between devices  27.3 us (45%)
  waiting for transfers between devices  22.3 us (37%)
  Pallas kernels  8.99 us (15%)
  between operations  0.89 us (1%)
  other arithmetic  0.84 us (1%)
    pallas_call x8, Pallas kernels, kernel_call(): pl.pallas_call(kernel, out_shape=out_shape, in_specs=specs, out_specs=[pl...  8.99 us
    ppermute x2, starting transfers between devices, shards(): kept_inner = [lax.ppermute(inner_kept, 'tm', pairs) for pairs in time_pairs]  8.04 us
    ppermute x2, waiting for transfers between devices, shards(): kept_inner = [lax.ppermute(inner_kept, 'tm', pairs) for pairs in time_pairs]  6.81 us
    ppermute x2, starting transfers between devices, shards(): first_edge = [lax.ppermute(edge_away, 'tm', pairs) for pairs in time_pairs]  6.6 us
    ppermute x1, waiting for transfers between devices, shards(): arrived = lax.ppermute(sent, 'net', swaps(lax.axis_size('net'), 0))  5.51 us
    ppermute x2, waiting for transfers between devices, shards(): lax.ppermute(inner_away, 'tm', pairs)  5.04 us
    ppermute x2, waiting for transfers between devices, shards(): kept_edge = [lax.ppermute(edge_kept, 'tm', pairs) for pairs in time_pairs]  4.93 us
    ppermute x2, starting transfers between devices, shards(): kept_edge = [lax.ppermute(edge_kept, 'tm', pairs) for pairs in time_pairs]  3.56 us
  transfers between devices with their start and end apart: 15, of which 4 were waited for; matrix products, arithmetic and copies ran while one was open for 0% of the time, Pallas kernels for 13%

profile of v2, /device:TPU:0, one launch (start us, length us, event | category | flops | bytes accessed | tf_op | source)
XLA Modules:
  0.0 60.4 jit_solution(559494754087440438)
XLA Ops:
  0.0 1.2 %shard_map.77 = (bf16[2,64,1280]{2,1,0:T(8,128)(2,1)S(1)}, bf16[2,64,1280]{2,1,0:T(8,128)(2,1)S(1)}) custom-call(bf16[2,64,2560]{2,1,0:T(8,128)(2,1)} %bitcast.12, bf16[2,64,2560]{2,1,0:T(8,128)(2,1)} %bitcast.16), custom_call_target="tpu_custom_call" | custom-call | tf_op jit(solution)/shard_map/pallas_call | solution.py:25
  1.2 0.7 %collective-permute-start.8 = (bf16[2,64,1280]{2,1,0:T(8,128)(2,1)S(1)}, bf16[2,64,1280]{2,1,0:T(8,128)(2,1)S(1)}, u32[]{:S(2)}, u32[]{:S(2)}) collective-permute-start(bf16[2,64,1280]{2,1,0:T(8,128)(2,1)S(1)} %get-tuple-element.17), channel_id=1, source_target_pairs={{8,16},{16,8},{9,17},{17,9},{10,18},{18,10},{11,19},{19,11},{12,20... | collective-permute-start | bytes 983048 | tf_op jit(solution)/shard_map/ppermute | solution.py:219
  1.9 5.9 %collective-permute-start.9 = (bf16[2,64,1280]{2,1,0:T(8,128)(2,1)S(1)}, bf16[2,64,1280]{2,1,0:T(8,128)(2,1)S(1)}, u32[]{:S(2)}, u32[]{:S(2)}) collective-permute-start(bf16[2,64,1280]{2,1,0:T(8,128)(2,1)S(1)} %get-tuple-element.17), channel_id=1, source_target_pairs={{0,8},{16,24},{8,0},{24,16},{1,9},{17,25},{9,1},{25,17},{2,10},{18... | collective-permute-start | bytes 983048 | tf_op jit(solution)/shard_map/ppermute | solution.py:219
  7.8 0.7 %collective-permute-start.10 = (bf16[2,64,1280]{2,1,0:T(8,128)(2,1)S(1)}, bf16[2,64,1280]{2,1,0:T(8,128)(2,1)S(1)}, u32[]{:S(2)}, u32[]{:S(2)}) collective-permute-start(bf16[2,64,1280]{2,1,0:T(8,128)(2,1)S(1)} %get-tuple-element.18), channel_id=1, source_target_pairs={{8,16},{16,8},{9,17},{17,9},{10,18},{18,10},{11,19},{19,11},{12,20... | collective-permute-start | bytes 983048 | tf_op jit(solution)/shard_map/ppermute | solution.py:220
  8.5 1.8 %collective-permute-start.11 = (bf16[2,64,1280]{2,1,0:T(8,128)(2,1)S(1)}, bf16[2,64,1280]{2,1,0:T(8,128)(2,1)S(1)}, u32[]{:S(2)}, u32[]{:S(2)}) collective-permute-start(bf16[2,64,1280]{2,1,0:T(8,128)(2,1)S(1)} %get-tuple-element.18), channel_id=1, source_target_pairs={{0,8},{16,24},{8,0},{24,16},{1,9},{17,25},{9,1},{25,17},{2,10},{18... | collective-permute-start | bytes 983048 | tf_op jit(solution)/shard_map/ppermute | solution.py:220
  11.0 2.3 %shard_map.73 = (bf16[2,64,2560]{2,1,0:T(8,128)(2,1)S(1)}, bf16[2,64,2560]{2,1,0:T(8,128)(2,1)S(1)}, bf16[2,64,1280]{2,1,0:T(8,128)(2,1)S(1)}, bf16[2,64,1280]{2,1,0:T(8,128)(2,1)S(1)}, f32[1,2560]{1,0:T(1,128)S(1)}) custom-call(bf16[2,64,2560]{2,1,0:T(8,128)(2,1)} %bitcast.13, bf16[2,64,2560]{2,1,0:T(8,128)(2,1)} %bitcast.17, ...), custom_call_target="tpu_custom_call" | custom-call | tf_op jit(solution)/shard_map/pallas_call | solution.py:25
  13.3 0.7 %collective-permute-start.2 = (bf16[2,64,1280]{2,1,0:T(8,128)(2,1)S(1)}, bf16[2,64,1280]{2,1,0:T(8,128)(2,1)S(1)}, u32[]{:S(2)}, u32[]{:S(2)}) collective-permute-start(bf16[2,64,1280]{2,1,0:T(8,128)(2,1)S(1)} %get-tuple-element.15), channel_id=1, source_target_pairs={{8,16},{16,8},{9,17},{17,9},{10,18},{18,10},{11,19},{19,11},{12,20... | collective-permute-start | bytes 983048 | tf_op jit(solution)/shard_map/ppermute | solution.py:227
  14.0 2.9 %collective-permute-start.3 = (bf16[2,64,1280]{2,1,0:T(8,128)(2,1)S(1)}, bf16[2,64,1280]{2,1,0:T(8,128)(2,1)S(1)}, u32[]{:S(2)}, u32[]{:S(2)}) collective-permute-start(bf16[2,64,1280]{2,1,0:T(8,128)(2,1)S(1)} %get-tuple-element.15), channel_id=1, source_target_pairs={{0,8},{16,24},{8,0},{24,16},{1,9},{17,25},{9,1},{25,17},{2,10},{18... | collective-permute-start | bytes 983048 | tf_op jit(solution)/shard_map/ppermute | solution.py:227
  16.9 0.7 %collective-permute-start.4 = (bf16[2,64,1280]{2,1,0:T(8,128)(2,1)S(1)}, bf16[2,64,1280]{2,1,0:T(8,128)(2,1)S(1)}, u32[]{:S(2)}, u32[]{:S(2)}) collective-permute-start(bf16[2,64,1280]{2,1,0:T(8,128)(2,1)S(1)} %get-tuple-element.16), channel_id=1, source_target_pairs={{8,16},{16,8},{9,17},{17,9},{10,18},{18,10},{11,19},{19,11},{12,20... | collective-permute-start | bytes 983048 | tf_op jit(solution)/shard_map/ppermute | solution.py:228
  17.6 0.7 %collective-permute-start = (bf16[2,64,2560]{2,1,0:T(8,128)(2,1)S(1)}, bf16[2,64,2560]{2,1,0:T(8,128)(2,1)S(1)}, u32[]{:S(2)}, u32[]{:S(2)}) collective-permute-start(bf16[2,64,2560]{2,1,0:T(8,128)(2,1)S(1)} %get-tuple-element.13), channel_id=1, source_target_pairs={{2,4},{4,2},{3,5},{5,3},{10,12},{12,10},{11,13},{13,11},{18,20},{2... | collective-permute-start | bytes 1966088 | tf_op jit(solution)/shard_map/ppermute | solution.py:225
  18.4 5.0 %collective-permute-done.11.even_ref.even_inner_ref = bf16[2,64,1280]{2,1,0:T(8,128)(2,1)S(1)} collective-permute-done((bf16[2,64,1280]{2,1,0:T(8,128)(2,1)S(1)}, bf16[2,64,1280]{2,1,0:T(8,128)(2,1)S(1)}, u32[]{:S(2)}, u32[]{:S(2)}) %collective-permute-start.11) | collective-permute-done | bytes 327712 | tf_op jit(solution)/shard_map/ppermute | solution.py:220
  23.5 0.0 copy-start
  23.5 0.0 copy-start.3
  23.5 0.8 %collective-permute-start.12 = (bf16[2,2,64,1280]{3,2,1,0:T(8,128)(2,1)S(1)}, bf16[2,2,64,1280]{3,2,1,0:T(8,128)(2,1)S(1)}, u32[]{:S(2)}, u32[]{:S(2)}) collective-permute-start(bf16[2,2,64,1280]{3,2,1,0:T(8,128)(2,1)S(1)} %shard_map.78), channel_id=1, source_target_pairs={{2,4},{4,2},{3,5},{5,3},{10,12},{12,10},{11,13},{13,11},{18,20},{2... | collective-permute-start | bytes 1966088 | tf_op jit(solution)/shard_map/ppermute | solution.py:233
  24.4 4.9 %collective-permute-done.3.even_ref.even_edge_ref = bf16[2,64,1280]{2,1,0:T(8,128)(2,1)S(1)} collective-permute-done((bf16[2,64,1280]{2,1,0:T(8,128)(2,1)S(1)}, bf16[2,64,1280]{2,1,0:T(8,128)(2,1)S(1)}, u32[]{:S(2)}, u32[]{:S(2)}) %collective-permute-start.3) | collective-permute-done | bytes 327712 | tf_op jit(solution)/shard_map/ppermute | solution.py:227
  29.3 7.4 %collective-permute-start.5 = (bf16[2,64,1280]{2,1,0:T(8,128)(2,1)S(1)}, bf16[2,64,1280]{2,1,0:T(8,128)(2,1)S(1)}, u32[]{:S(2)}, u32[]{:S(2)}) collective-permute-start(bf16[2,64,1280]{2,1,0:T(8,128)(2,1)S(1)} %get-tuple-element.16), channel_id=1, source_target_pairs={{0,8},{16,24},{8,0},{24,16},{1,9},{17,25},{9,1},{25,17},{2,10},{18... | collective-permute-start | bytes 983048 | tf_op jit(solution)/shard_map/ppermute | solution.py:228
  36.7 6.8 %collective-permute-done.5.even_ref.even_inner_ref = bf16[2,64,1280]{2,1,0:T(8,128)(2,1)S(1)} collective-permute-done((bf16[2,64,1280]{2,1,0:T(8,128)(2,1)S(1)}, bf16[2,64,1280]{2,1,0:T(8,128)(2,1)S(1)}, u32[]{:S(2)}, u32[]{:S(2)}) %collective-permute-start.5) | collective-permute-done | bytes 327712 | tf_op jit(solution)/shard_map/ppermute | solution.py:228
  43.5 0.7 %collective-permute-start.6 = (bf16[2,2,64,1280]{3,2,1,0:T(8,128)(2,1)S(1)}, bf16[2,2,64,1280]{3,2,1,0:T(8,128)(2,1)S(1)}, u32[]{:S(2)}, u32[]{:S(2)}) collective-permute-start(bf16[2,2,64,1280]{3,2,1,0:T(8,128)(2,1)S(1)} %shard_map.74), channel_id=1, source_target_pairs={{2,4},{4,2},{3,5},{5,3},{10,12},{12,10},{11,13},{13,11},{18,20},{2... | collective-permute-start | bytes 1966088 | tf_op jit(solution)/shard_map/ppermute | solution.py:240
  44.3 2.9 %collective-permute-start.7 = (bf16[2,2,64,1280]{3,2,1,0:T(8,128)(2,1)S(1)}, bf16[2,2,64,1280]{3,2,1,0:T(8,128)(2,1)S(1)}, u32[]{:S(2)}, u32[]{:S(2)}) collective-permute-start(bf16[2,2,64,1280]{3,2,1,0:T(8,128)(2,1)S(1)} %shard_map.75), channel_id=1, source_target_pairs={{0,2},{4,6},{2,0},{6,4},{1,3},{5,7},{3,1},{7,5},{8,10},{12,14},{10... | collective-permute-start | bytes 1966088 | tf_op jit(solution)/shard_map/ppermute | solution.py:241
  47.3 2.7 %shard_map.80 = bf16[2,64,1280]{2,1,0:T(8,128)(2,1)S(1)} custom-call(s32[2,9]{1,0:T(2,128)S(1)} %bitcast.22, s32[1,2]{1,0:T(1,128)S(1)} %copy-done.4, f32[1,2560]{1,0:T(1,128)S(1)} %get-tuple-element.12.gate_ref, bf16[2,64,2560]{2,1,0:T(8,128)(2,1)S(1)} %bitcast.20, bf16[2,64,2560]{2,1,0:T(8,128)(2,1)S(1)} %bitcast.14, bf16[2,64,2560]{2,1,0:T(8,128)(2,1)S(1)} %bitcast.18, ...), custom_call_target="tpu_custom_call" | custom-call | flops 503316480 | bytes 3932160 | tf_op jit(solution)/shard_map/pallas_call | solution.py:25
  49.9 1.6 %collective-permute-start.14 = (bf16[2,64,1280]{2,1,0:T(8,128)(2,1)S(1)}, bf16[2,64,1280]{2,1,0:T(8,128)(2,1)S(1)}, u32[]{:S(2)}, u32[]{:S(2)}) collective-permute-start(bf16[2,64,1280]{2,1,0:T(8,128)(2,1)S(1)} %shard_map.80), channel_id=1, source_target_pairs={{0,1},{1,0},{2,3},{3,2},{4,5},{5,4},{6,7},{7,6},{8,9},{9,8},{10,11... | collective-permute-start | bytes 983048 | tf_op jit(solution)/shard_map/ppermute | solution.py:239
  51.5 2.6 %shard_map.76 = f32[2,64,1280]{2,1,0:T(8,128)S(1)} custom-call(s32[2,9]{1,0:T(2,128)S(1)} %bitcast.23, s32[1,2]{1,0:T(1,128)S(1)} %copy-done.4, f32[1,2560]{1,0:T(1,128)S(1)} %get-tuple-element.12.gate_ref, bf16[2,64,2560]{2,1,0:T(8,128)(2,1)S(1)} %bitcast.21, bf16[2,64,2560]{2,1,0:T(8,128)(2,1)S(1)} %bitcast.15, bf16[2,64,2560]{2,1,0:T(8,128)(2,1)S(1)} %bitcast.19, ...), custom_call_target="tpu_custom_call" | custom-call | flops 503316480 | bytes 3932160 | tf_op jit(solution)/shard_map/pallas_call | solution.py:25
  54.1 5.5 %collective-permute-done.14 = bf16[2,64,1280]{2,1,0:T(8,128)(2,1)S(1)} collective-permute-done((bf16[2,64,1280]{2,1,0:T(8,128)(2,1)S(1)}, bf16[2,64,1280]{2,1,0:T(8,128)(2,1)S(1)}, u32[]{:S(2)}, u32[]{:S(2)}) %collective-permute-start.14) | collective-permute-done | bytes 327712 | tf_op jit(solution)/shard_map/ppermute | solution.py:239
  59.6 0.8 %fusion = bf16[1,2,64,1280]{3,2,1,0:T(8,128)(2,1)} fusion(f32[2,64,1280]{2,1,0:T(8,128)S(1)} %shard_map.76, bf16[2,64,1280]{2,1,0:T(8,128)(2,1)S(1)} %collective-permute-done.14), kind=kLoop, calls=%fused_computation.1 | loop fusion | flops 491520 | bytes 1310720 | tf_op jit(solution)/shard_map/broadcast_in_dim | solution.py:246
  (27 shorter events, 0.3 us)
Async XLA Ops:
  1.2 12.8 %collective-permute-start.8 = (bf16[2,64,1280]{2,1,0:T(8,128)(2,1)S(1)}, bf16[2,64,1280]{2,1,0:T(8,128)(2,1)S(1)}, u32[]{:S(2)}, u32[]{:S(2)}) collective-permute-start(bf16[2,64,1280]{2,1,0:T(8,128)(2,1)S(1)} %get-tuple-element.17), channel_id=1, source_target_pairs={{8,16},{16,8},{9,17},{17,9},{10,18},{18,10},{11,19},{19,11},{12,20... | collective-permute-start | bytes 983048 | tf_op jit(solution)/shard_map/ppermute | solution.py:219
  1.9 15.0 %collective-permute-start.9 = (bf16[2,64,1280]{2,1,0:T(8,128)(2,1)S(1)}, bf16[2,64,1280]{2,1,0:T(8,128)(2,1)S(1)}, u32[]{:S(2)}, u32[]{:S(2)}) collective-permute-start(bf16[2,64,1280]{2,1,0:T(8,128)(2,1)S(1)} %get-tuple-element.17), channel_id=1, source_target_pairs={{0,8},{16,24},{8,0},{24,16},{1,9},{17,25},{9,1},{25,17},{2,10},{18... | collective-permute-start | bytes 983048 | tf_op jit(solution)/shard_map/ppermute | solution.py:219
  7.8 9.8 %collective-permute-start.10 = (bf16[2,64,1280]{2,1,0:T(8,128)(2,1)S(1)}, bf16[2,64,1280]{2,1,0:T(8,128)(2,1)S(1)}, u32[]{:S(2)}, u32[]{:S(2)}) collective-permute-start(bf16[2,64,1280]{2,1,0:T(8,128)(2,1)S(1)} %get-tuple-element.18), channel_id=1, source_target_pairs={{8,16},{16,8},{9,17},{17,9},{10,18},{18,10},{11,19},{19,11},{12,20... | collective-permute-start | bytes 983048 | tf_op jit(solution)/shard_map/ppermute | solution.py:220
  8.5 14.9 %collective-permute-start.11 = (bf16[2,64,1280]{2,1,0:T(8,128)(2,1)S(1)}, bf16[2,64,1280]{2,1,0:T(8,128)(2,1)S(1)}, u32[]{:S(2)}, u32[]{:S(2)}) collective-permute-start(bf16[2,64,1280]{2,1,0:T(8,128)(2,1)S(1)} %get-tuple-element.18), channel_id=1, source_target_pairs={{0,8},{16,24},{8,0},{24,16},{1,9},{17,25},{9,1},{25,17},{2,10},{18... | collective-permute-start | bytes 983048 | tf_op jit(solution)/shard_map/ppermute | solution.py:220
  13.3 10.2 %collective-permute-start.2 = (bf16[2,64,1280]{2,1,0:T(8,128)(2,1)S(1)}, bf16[2,64,1280]{2,1,0:T(8,128)(2,1)S(1)}, u32[]{:S(2)}, u32[]{:S(2)}) collective-permute-start(bf16[2,64,1280]{2,1,0:T(8,128)(2,1)S(1)} %get-tuple-element.15), channel_id=1, source_target_pairs={{8,16},{16,8},{9,17},{17,9},{10,18},{18,10},{11,19},{19,11},{12,20... | collective-permute-start | bytes 983048 | tf_op jit(solution)/shard_map/ppermute | solution.py:227
  14.0 15.3 %collective-permute-start.3 = (bf16[2,64,1280]{2,1,0:T(8,128)(2,1)S(1)}, bf16[2,64,1280]{2,1,0:T(8,128)(2,1)S(1)}, u32[]{:S(2)}, u32[]{:S(2)}) collective-permute-start(bf16[2,64,1280]{2,1,0:T(8,128)(2,1)S(1)} %get-tuple-element.15), channel_id=1, source_target_pairs={{0,8},{16,24},{8,0},{24,16},{1,9},{17,25},{9,1},{25,17},{2,10},{18... | collective-permute-start | bytes 983048 | tf_op jit(solution)/shard_map/ppermute | solution.py:227
  16.9 12.4 %collective-permute-start.4 = (bf16[2,64,1280]{2,1,0:T(8,128)(2,1)S(1)}, bf16[2,64,1280]{2,1,0:T(8,128)(2,1)S(1)}, u32[]{:S(2)}, u32[]{:S(2)}) collective-permute-start(bf16[2,64,1280]{2,1,0:T(8,128)(2,1)S(1)} %get-tuple-element.16), channel_id=1, source_target_pairs={{8,16},{16,8},{9,17},{17,9},{10,18},{18,10},{11,19},{19,11},{12,20... | collective-permute-start | bytes 983048 | tf_op jit(solution)/shard_map/ppermute | solution.py:228
  17.6 26.7 %collective-permute-start = (bf16[2,64,2560]{2,1,0:T(8,128)(2,1)S(1)}, bf16[2,64,2560]{2,1,0:T(8,128)(2,1)S(1)}, u32[]{:S(2)}, u32[]{:S(2)}) collective-permute-start(bf16[2,64,2560]{2,1,0:T(8,128)(2,1)S(1)} %get-tuple-element.13), channel_id=1, source_target_pairs={{2,4},{4,2},{3,5},{5,3},{10,12},{12,10},{11,13},{13,11},{18,20},{2... | collective-permute-start | bytes 1966088 | tf_op jit(solution)/shard_map/ppermute | solution.py:225
  23.4 23.8 %collective-permute-start.1 = (bf16[2,64,2560]{2,1,0:T(8,128)(2,1)S(1)}, bf16[2,64,2560]{2,1,0:T(8,128)(2,1)S(1)}, u32[]{:S(2)}, u32[]{:S(2)}) collective-permute-start(bf16[2,64,2560]{2,1,0:T(8,128)(2,1)S(1)} %get-tuple-element.14), channel_id=1, source_target_pairs={{0,2},{4,6},{2,0},{6,4},{1,3},{5,7},{3,1},{7,5},{8,10},{12,14},{10... | collective-permute-start | bytes 1966088 | tf_op jit(solution)/shard_map/ppermute | solution.py:226
  23.5 23.8 %copy-start = (bf16[1,1,2,64,2560]{4,3,2,1,0:T(8,128)(2,1)S(1)}, bf16[1,1,2,64,2560]{4,3,2,1,0:T(8,128)(2,1)}, u32[]{:S(2)}) copy-start(bf16[1,1,2,64,2560]{4,3,2,1,0:T(8,128)(2,1)} %param.8) | copy-start | bytes 1966084
  23.5 23.8 %copy-start.1 = (bf16[1,1,2,64,2560]{4,3,2,1,0:T(8,128)(2,1)S(1)}, bf16[1,1,2,64,2560]{4,3,2,1,0:T(8,128)(2,1)}, u32[]{:S(2)}) copy-start(bf16[1,1,2,64,2560]{4,3,2,1,0:T(8,128)(2,1)} %param.9) | copy-start | bytes 1966084
  23.5 23.8 %copy-start.2 = (bf16[1,1,2,64,2560]{4,3,2,1,0:T(8,128)(2,1)S(1)}, bf16[1,1,2,64,2560]{4,3,2,1,0:T(8,128)(2,1)}, u32[]{:S(2)}) copy-start(bf16[1,1,2,64,2560]{4,3,2,1,0:T(8,128)(2,1)} %param.7) | copy-start | bytes 1966084
  23.5 23.7 %copy-start.3 = (s32[1,2,9]{2,1,0:T(2,128)S(1)}, s32[1,2,9]{2,1,0:T(2,128)}, u32[]{:S(2)}) copy-start(s32[1,2,9]{2,1,0:T(2,128)} %param.11) | copy-start | bytes 220
  23.5 23.7 %copy-start.4 = (s32[1,2]{1,0:T(1,128)S(1)}, s32[1,2]{1,0:T(1,128)}, u32[]{:S(2)}) copy-start(s32[1,2]{1,0:T(1,128)} %count_ref.3) | copy-start | bytes 28
  23.5 23.7 %collective-permute-start.12 = (bf16[2,2,64,1280]{3,2,1,0:T(8,128)(2,1)S(1)}, bf16[2,2,64,1280]{3,2,1,0:T(8,128)(2,1)S(1)}, u32[]{:S(2)}, u32[]{:S(2)}) collective-permute-start(bf16[2,2,64,1280]{3,2,1,0:T(8,128)(2,1)S(1)} %shard_map.78), channel_id=1, source_target_pairs={{2,4},{4,2},{3,5},{5,3},{10,12},{12,10},{11,13},{13,11},{18,20},{2... | collective-permute-start | bytes 1966088 | tf_op jit(solution)/shard_map/ppermute | solution.py:233
  29.3 17.9 %collective-permute-start.13 = (bf16[2,2,64,1280]{3,2,1,0:T(8,128)(2,1)S(1)}, bf16[2,2,64,1280]{3,2,1,0:T(8,128)(2,1)S(1)}, u32[]{:S(2)}, u32[]{:S(2)}) collective-permute-start(bf16[2,2,64,1280]{3,2,1,0:T(8,128)(2,1)S(1)} %shard_map.79), channel_id=1, source_target_pairs={{0,2},{4,6},{2,0},{6,4},{1,3},{5,7},{3,1},{7,5},{8,10},{12,14},{10... | collective-permute-start | bytes 1966088 | tf_op jit(solution)/shard_map/ppermute | solution.py:234
  29.3 14.2 %collective-permute-start.5 = (bf16[2,64,1280]{2,1,0:T(8,128)(2,1)S(1)}, bf16[2,64,1280]{2,1,0:T(8,128)(2,1)S(1)}, u32[]{:S(2)}, u32[]{:S(2)}) collective-permute-start(bf16[2,64,1280]{2,1,0:T(8,128)(2,1)S(1)} %get-tuple-element.16), channel_id=1, source_target_pairs={{0,8},{16,24},{8,0},{24,16},{1,9},{17,25},{9,1},{25,17},{2,10},{18... | collective-permute-start | bytes 983048 | tf_op jit(solution)/shard_map/ppermute | solution.py:228
  43.5 8.0 %collective-permute-start.6 = (bf16[2,2,64,1280]{3,2,1,0:T(8,128)(2,1)S(1)}, bf16[2,2,64,1280]{3,2,1,0:T(8,128)(2,1)S(1)}, u32[]{:S(2)}, u32[]{:S(2)}) collective-permute-start(bf16[2,2,64,1280]{3,2,1,0:T(8,128)(2,1)S(1)} %shard_map.74), channel_id=1, source_target_pairs={{2,4},{4,2},{3,5},{5,3},{10,12},{12,10},{11,13},{13,11},{18,20},{2... | collective-permute-start | bytes 1966088 | tf_op jit(solution)/shard_map/ppermute | solution.py:240
  44.3 7.2 %collective-permute-start.7 = (bf16[2,2,64,1280]{3,2,1,0:T(8,128)(2,1)S(1)}, bf16[2,2,64,1280]{3,2,1,0:T(8,128)(2,1)S(1)}, u32[]{:S(2)}, u32[]{:S(2)}) collective-permute-start(bf16[2,2,64,1280]{3,2,1,0:T(8,128)(2,1)S(1)} %shard_map.75), channel_id=1, source_target_pairs={{0,2},{4,6},{2,0},{6,4},{1,3},{5,7},{3,1},{7,5},{8,10},{12,14},{10... | collective-permute-start | bytes 1966088 | tf_op jit(solution)/shard_map/ppermute | solution.py:241
  49.9 9.7 %collective-permute-start.14 = (bf16[2,64,1280]{2,1,0:T(8,128)(2,1)S(1)}, bf16[2,64,1280]{2,1,0:T(8,128)(2,1)S(1)}, u32[]{:S(2)}, u32[]{:S(2)}) collective-permute-start(bf16[2,64,1280]{2,1,0:T(8,128)(2,1)S(1)} %shard_map.80), channel_id=1, source_target_pairs={{0,1},{1,0},{2,3},{3,2},{4,5},{5,4},{6,7},{7,6},{8,9},{9,8},{10,11... | collective-permute-start | bytes 983048 | tf_op jit(solution)/shard_map/ppermute | solution.py:239
